TPU v7x, 128 devices: a whole 4x4x4 slice. The times are simulated.
128 devices in a mesh: tm: 8 (over y_lo, z), py: 4 (over x), pz: 4 (over y_hi, core).
Axes of the slice: x: 4, y: 4 (y_hi: 2, y_lo: 2; y = y_hi * 2 + y_lo), z: 4, core: 2. Of those that a mesh axis runs over, the one named last changes fastest.
Arguments:
- state_old: float32 [8, 4, 128, 128, 128], P('tm', None, 'py', 'pz'), may hold values from -6 to 6
Outputs:
- new_states: float32 [8, 4, 128, 128, 128], P('tm', None, 'py', 'pz')
All inputs are finite; a program needn't handle non-finite values.
Results may differ from a plain program's by a relative error of at most 0.00017.
Values sent between devices are 32-bit elements; how exact they have to be, the bound alone decides.
A program may use at most 128 MiB of HBM per device.

v0:
```python
import jax
import jax.numpy as jnp
from jax import lax
from jax.sharding import PartitionSpec as P

KMAX = 42
KCO = 21


time_step = 0.01
coriolis = 6.0
buoyancy_square = 100.0
viscosity = 0.001
diffusivity = 0.001


def items_in_groups(value, axis, split_dim, concat_dim, work, item_dim, out_dim):
    items = jax.tree.leaves(value)[0].shape[item_dim]
    count = 2 if items % 2 == 0 else 1
    outs = []
    for k in range(count):
        group = jax.tree.map(
            lambda a: lax.slice_in_dim(
                a, k * (items // count), (k + 1) * (items // count), axis=item_dim
            ),
            value,
        )
        outs.append(
            work(
                lax.all_to_all(
                    group, axis, split_axis=split_dim, concat_axis=concat_dim, tiled=True
                )
            )
        )
    return jax.tree.map(lambda *parts: jnp.concatenate(parts, axis=out_dim), *outs)


def passed_along(value, axis, by):
    length = lax.axis_size(axis)
    pairs = [(i, i + by) for i in range(length) if 0 <= i + by < length]
    return lax.ppermute(value, axis, pairs)


def product(form, left, right):
    return jnp.einsum(
        form, left, right, precision=lax.Precision.HIGHEST, preferred_element_type=jnp.float32
    )


def radians(waves, extent):
    cells = jnp.arange(extent)
    return 2.0 * jnp.pi / extent * (waves[:, None] * cells[None, :] % extent).astype(jnp.float32)


def first_tables(slots, extent):
    waves = jnp.arange(slots)
    inside = (waves <= KMAX).astype(jnp.float32)[:, None]
    angle = radians(waves, extent)
    scale = extent ** (-0.5)
    forward = jnp.stack([jnp.cos(angle), -jnp.sin(angle)]) * (inside * scale)
    weight = jnp.where(waves == 0, 1.0, 2.0).astype(jnp.float32)[:, None] * inside * scale
    backward = jnp.stack([jnp.cos(angle), -jnp.sin(angle)]) * weight
    return (forward, backward)


def complex_block(real_part, imag_part):
    upper = jnp.stack([real_part, imag_part], axis=1)
    lower = jnp.stack([-imag_part, real_part], axis=1)
    return jnp.stack([upper, lower])


def other_tables(slots, extent):
    waves = jnp.arange(slots) - KMAX
    inside = (waves <= KMAX).astype(jnp.float32)[:, None]
    angle = radians(waves, extent)
    scale = extent ** (-0.5)
    cosine = jnp.cos(angle) * inside * scale
    sine = jnp.sin(angle) * inside * scale
    return (complex_block(cosine.T, -sine.T), complex_block(cosine, sine))


def wave_parts(first_index, second_index, third_slots):
    wave_x = first_index.astype(jnp.float32)[:, None, None]
    wave_y = (second_index - KMAX).astype(jnp.float32)[None, :, None]
    third = (third_slots - KMAX).astype(jnp.float32)
    third = jnp.concatenate([third, third])
    return (wave_x, wave_y, third[None, None, :])


def coarse_inside(waves):
    wave_x, wave_y, wave_z = waves
    return (wave_x <= KCO) & (jnp.abs(wave_y) <= KCO) & (jnp.abs(wave_z) <= KCO)


def times_i(values):
    half = values.shape[-1] // 2
    return jnp.concatenate([-values[..., half:], values[..., :half]], axis=-1)


def squared(waves):
    wave_x, wave_y, wave_z = waves
    return wave_x**2 + wave_y**2 + wave_z**2


def project(velocity, waves):
    wave_x, wave_y, wave_z = waves
    along = (wave_x * velocity[0] + wave_y * velocity[1] + wave_z * velocity[2]) / jnp.maximum(
        squared(waves), 1.0
    )
    return (
        velocity[0] - wave_x * along,
        velocity[1] - wave_y * along,
        velocity[2] - wave_z * along,
    )


def linear(state, waves):
    square = squared(waves)
    pushed = project((coriolis * state[1], -coriolis * state[0], state[3]), waves)
    return jnp.stack(
        [
            pushed[0] - viscosity * square * state[0],
            pushed[1] - viscosity * square * state[1],
            pushed[2] - viscosity * square * state[2],
            -buoyancy_square * state[2] - diffusivity * square * state[3],
        ]
    )


def propagate(state, waves):
    for half_step in range(2):
        anchor = state
        for order in (4.0, 3.0, 2.0, 1.0):
            state = anchor + 0.5 * time_step / order * linear(state, waves)
    return state


def rate(state, waves, to_grid, to_modes):
    wave_x, wave_y, wave_z = waves
    square = squared(waves)
    spin = jnp.stack(
        [
            times_i(wave_y * state[2] - wave_z * state[1]),
            times_i(wave_z * state[0] - wave_x * state[2]),
            times_i(wave_x * state[1] - wave_y * state[0]),
        ]
    )
    fields = to_grid(jnp.concatenate([state, spin]))
    speed_x, speed_y, speed_z, lift = (fields[0], fields[1], fields[2], fields[3])
    spin_x, spin_y, spin_z = (fields[4], fields[5], fields[6])
    products = jnp.stack(
        [
            speed_y * spin_z - speed_z * spin_y,
            speed_z * spin_x - speed_x * spin_z,
            speed_x * spin_y - speed_y * spin_x,
            speed_x * lift,
            speed_y * lift,
            speed_z * lift,
        ]
    )
    modes = to_modes(products)
    pushed = project(
        (modes[0] + coriolis * state[1], modes[1] - coriolis * state[0], modes[2] + state[3]), waves
    )
    lift_rate = (
        -times_i(wave_x * modes[3] + wave_y * modes[4] + wave_z * modes[5])
        - buoyancy_square * state[2]
        - diffusivity * square * state[3]
    )
    return jnp.stack(
        [
            pushed[0] - viscosity * square * state[0],
            pushed[1] - viscosity * square * state[1],
            pushed[2] - viscosity * square * state[2],
            lift_rate,
        ]
    )


def on_device(state_old):
    fields_grid = state_old[0]
    extent = fields_grid.shape[-1]
    rows_y, rows_z = (fields_grid.shape[1], fields_grid.shape[2])
    across_y = lax.axis_size("py")
    across_z = lax.axis_size("pz")
    joint = across_y * across_z
    first_slots = (KMAX + joint) // joint * joint
    other_slots = (2 * KMAX + across_z) // across_z * across_z
    fore_first, back_first = first_tables(first_slots, extent)
    fore_other, back_other = other_tables(other_slots, extent)
    width_x = first_slots // joint
    first_index = lax.axis_index(("py", "pz")) * width_x + jnp.arange(width_x)
    second_index = jnp.arange(other_slots)
    fore_y_blocks = fore_other.reshape(2, across_y, rows_y, 2, other_slots)
    fore_z_blocks = fore_other.reshape(2, across_z, rows_z, 2, other_slots)
    back_y_blocks = back_other.reshape(2, other_slots, 2, across_y, rows_y)

    def to_modes(physical):
        spread = product("fyzx,cax->fcayz", physical, fore_first)[None]

        def last_step(arrived):
            count = arrived.shape[1]
            blocks = arrived.reshape(across_y, across_z, count, 2, width_x, rows_y, rows_z)
            along_y = product("jkfcayz,cjyeb->kfeabz", blocks, fore_y_blocks)
            along_z = product("kfeabz,ekzgd->fabgd", along_y, fore_z_blocks)
            return along_z.reshape(count, width_x, other_slots, 2 * other_slots)

        return items_in_groups(spread, ("py", "pz"), 3, 0, last_step, 1, 0)

    def to_grid(modes):
        count = modes.shape[0]
        view = modes.reshape(count, width_x, other_slots, 2, other_slots)
        along_z = product("fabck,ckez->feabz", view, back_other)
        along_z = along_z.reshape(count, 2, width_x, other_slots, across_z, rows_z)
        blocks = product("feabkm,ebgjl->jkfgalm", along_z, back_y_blocks)
        blocks = blocks.reshape(joint, count, 2, width_x, rows_y, rows_z)

        def last_step(received):
            return product("ofcayz,cax->fyzx", received, back_first)

        return last_step(
            lax.all_to_all(blocks, ("py", "pz"), split_axis=0, concat_axis=3, tiled=True)
        )

    waves = wave_parts(first_index, second_index, jnp.arange(other_slots))
    start = to_modes(fields_grid)
    velocity = project((start[0], start[1], start[2]), waves)
    start = jnp.concatenate([jnp.stack(velocity), start[3:]])
    fine = start + time_step * rate(start, waves, to_grid, to_modes)
    band_slots = jnp.arange(other_slots)
    chain_waves = wave_parts(first_index, second_index, band_slots)
    keep = coarse_inside(chain_waves).astype(jnp.float32)
    later_slice = lax.axis_index("tm") > 0
    local = keep * fine - jnp.where(later_slice, keep * propagate(start, chain_waves), 0.0)

    def relay(turn, carry):
        arrived = passed_along(carry, "tm", 1)
        return local + keep * propagate(arrived, chain_waves)

    carry = lax.fori_loop(0, lax.axis_size("tm") - 1, relay, local)
    merged = jnp.where(coarse_inside(waves), carry, fine)
    return to_grid(merged)[None]


def solution(mesh):
    return jax.shard_map(
        on_device,
        mesh=mesh,
        in_specs=(P("tm", None, "py", "pz", None),),
        out_specs=P("tm", None, "py", "pz", None),
        check_vma=False,
    )
```

profile of v0, /device:TPU:8, one launch (start us, length us, event | category | flops | bytes accessed | tf_op | source)
XLA Modules:
  0.0 629.8 jit_solution(16473109906824881334)
XLA Ops:
  1.6 3.5 convolution_bitcast_fusion.2
  7.9 4.0 copy.87
  14.1 6.2 all-to-all-start.1
  20.4 4.0 copy.81
  27.4 8.1 %all-to-all-done.1 = f32[16,1,12288]{2,1,0:T(1,128)} async-done(((f32[16,1,12288]{2,1,0:T(1,128)}), f32[16,1,12288]{2,1,0:T(1,128)}, u32[]{:S(2)}, u32[]{:S(2)}) %all-to-all-start.1) | async-done | bytes 786464 | tf_op jit(solution)/shard_map/all_to_all | solution.py:30
  35.6 4.5 all-to-all-start
  42.6 4.5 reduce.5
  49.6 5.2 fusion.130
  57.0 4.5 reduce.4
  63.9 5.6 fusion.127
  83.7 10.5 %convolution_bitcast_fusion = f32[4,4,7,2,3,32,32]{6,5,1,4,2,0,3:T(8,128)S(1)} fusion(f32[7,2,3,88,4,32,1,1]{3,5,4,2,1,0,7,6:T(8,128)} %bitcast.382, f32[1,88,1,4,32]{1,4,0,3,2:T(8,128)S(1)} %copy-done.29, f32[1,88,1,4,32]{1,4,0,3,2:T(8,128)S(1)} %copy-done.27, f32[1,88,1,4,32]{1,4,0,3,2:T(8,128)S(1)} %copy-done.25), kind=kOutput, calls=%fused_computation.115 | convolution fusion | flops 1453461504 | bytes 4780032 | tf_op jit(solution)/shard_map/feabkm,ebgjl->jkfgalm/dot_general | solution.py:45
  94.3 6.1 copy.101
  100.3 9.8 %reshape.1385 = f32[16,1,43008]{2,1,0:T(1,128)} reshape(f32[16,7,2,3,32,32]{5,4,3,2,1,0:T(8,128)} %bitcast.364) | data formatting | bytes 5505024
  110.2 7.3 %all-to-all-start.2 = ((f32[16,1,43008]{2,1,0:T(1,128)}), f32[16,1,43008]{2,1,0:T(1,128)S(1)}, u32[]{:S(2)}, u32[]{:S(2)}) async-start(f32[16,1,43008]{2,1,0:T(1,128)} %reshape.1385), calls=%async_computation.2 | async-start | bytes 5505024 | tf_op jit(solution)/shard_map/all_to_all | solution.py:222
  117.5 36.2 %all-to-all-done.2 = f32[16,1,43008]{2,1,0:T(1,128)S(1)} async-done(((f32[16,1,43008]{2,1,0:T(1,128)}), f32[16,1,43008]{2,1,0:T(1,128)S(1)}, u32[]{:S(2)}, u32[]{:S(2)}) %all-to-all-start.2) | async-done | bytes 2752544 | tf_op jit(solution)/shard_map/all_to_all | solution.py:222
  153.8 9.6 %reduce.6 = f32[16,43008]{1,0:T(8,128)} reduce(f32[16,1,43008]{2,1,0:T(1,128)S(1)} %all-to-all-done.2, f32[]{:T(128)} %broadcast.2745), dimensions={1}, to_apply=%all_to_all.72.reduce_sub_computation | reduce | bytes 5505028 | tf_op jit(solution)/shard_map/all_to_all | solution.py:222
  163.3 11.5 %reshape.1386 = f32[16,7,2,3,32,32]{5,4,3,2,1,0:T(8,128)} reshape(f32[16,43008]{1,0:T(8,128)} %reduce.6) | data formatting | bytes 5505024
  174.8 6.1 copy.102
  180.9 21.4 %fusion.110 = f32[7,32,32,128]{3,2,1,0:T(8,128)S(1)} fusion(f32[7,2,48,32,32]{4,3,2,1,0:T(8,128)S(1)} %bitcast.366, f32[48]{0:T(128)S(1)} %fusion.265, f32[1,48,128]{2,1,0:T(8,128)S(1)} %get-tuple-element.391, f32[1,48,128]{2,1,0:T(8,128)S(1)} %get-tuple-element.392), kind=kOutput, calls=%fused_computation.126 | convolution fusion | flops 1056989184 | bytes 6471872 | tf_op jit(solution)/shard_map/ofcayz,cax->fyzx/dot_general | solution.py:45
  203.2 5.8 fusion.106
  211.4 6.6 %copy.104 = f32[1,3,2,48,32,32]{5,4,1,2,0,3:T(8,128)} copy(f32[1,3,2,48,32,32]{3,5,4,1,2,0:T(8,128)} %get-tuple-element.322) | data formatting | bytes 2359296 | tf_op jit(solution)/shard_map/slice | solution.py:23
  218.0 5.0 reshape.1389
  223.1 7.3 %all-to-all-start.3 = ((f32[16,1,18432]{2,1,0:T(1,128)}), f32[16,1,18432]{2,1,0:T(1,128)}, u32[]{:S(2)}, u32[]{:S(2)}) async-start(f32[16,1,18432]{2,1,0:T(1,128)} %reshape.1389), calls=%async_computation.3 | async-start | bytes 2359296 | tf_op jit(solution)/shard_map/all_to_all | solution.py:30
  230.6 5.0 copy.111
  235.5 5.0 reshape.1387
  240.5 9.3 %all-to-all-done.3 = f32[16,1,18432]{2,1,0:T(1,128)} async-done(((f32[16,1,18432]{2,1,0:T(1,128)}), f32[16,1,18432]{2,1,0:T(1,128)}, u32[]{:S(2)}, u32[]{:S(2)}) %all-to-all-start.3) | async-done | bytes 1179680 | tf_op jit(solution)/shard_map/all_to_all | solution.py:30
  249.8 3.7 all-to-all-start.4
  254.6 5.7 reduce.8
  260.3 4.2 reshape.1390
  267.5 7.6 %fusion.121 = f32[4,3,2,3,88,32,1]{4,5,0,2,6,3,1:T(8,128)S(1)} fusion(f32[4,4,3,2,3,32,32,1]{6,5,4,1,0,3,2,7:T(8,128)S(1)} %bitcast.371, f32[1,4,32,1,88]{4,2,1,0,3:T(8,128)S(1)} %get-tuple-element.383, f32[1,4,32,1,88]{4,2,1,0,3:T(8,128)S(1)} %get-tuple-element.382, f32[1,4,32,1,88]{4,2,1,0,3:T(8,128)S(1)} %get-tuple-element.381), kind=kOutput, calls=%fused_computation.131 | convolution fusion | flops 622989312 | bytes 2125824 | tf_op jit(solution)/shard_map/jkfcayz,cjyeb->kfeabz/dot_general | solution.py:45
  279.4 4.7 reduce.7
  284.1 4.2 reshape.1388
  291.4 7.6 %fusion.124 = f32[4,3,2,3,88,32,1]{4,5,0,2,6,3,1:T(8,128)S(1)} fusion(f32[4,4,3,2,3,32,32,1]{6,5,4,1,0,3,2,7:T(8,128)S(1)} %bitcast.373, f32[1,4,32,1,88]{4,2,1,0,3:T(8,128)S(1)} %get-tuple-element.383, f32[1,4,32,1,88]{4,2,1,0,3:T(8,128)S(1)} %get-tuple-element.382, f32[1,4,32,1,88]{4,2,1,0,3:T(8,128)S(1)} %get-tuple-element.381), kind=kOutput, calls=%fused_computation.132 | convolution fusion | flops 622989312 | bytes 2125824 | tf_op jit(solution)/shard_map/jkfcayz,cjyeb->kfeabz/dot_general | solution.py:45
  312.3 243.5 %while.14 = (s32[]{:T(128)}, f32[4,3,88,176]{3,2,1,0:T(8,128)}, f32[1,1,176]{2,1,0:T(1,128)S(1)}, f32[1,1,176]{2,1,0:T(1,128)S(1)}, f32[4,3,88,176]{3,2,1,0:T(8,...) while((s32[]{:T(128)}, f32[4,3,88,176]{3,2,1,0:T(8,128)}, ...), condition=%wide.region_1.2_spmd.clone.clone.clone, body=%wide.region_0.1_spmd.clone.clone.clone.sunk | while | flops 22024928 | bytes 44282072 | solution.py:240
  312.3 3.8 collective-permute-start
  316.4 27.1 %collective-permute-done = f32[4,3,88,176]{3,2,1,0:T(8,128)S(1)} collective-permute-done((f32[4,3,88,176]{3,2,1,0:T(8,128)}, f32[4,3,88,176]{3,2,1,0:T(8,128)S(1)}, u32[]{:S(2)}, u32[]{:S(2)}) %collective-permute-start) | collective-permute-done | bytes 743456 | tf_op jit(solution)/shard_map/while/body/eval_jaxpr/ppermute | solution.py:41
  352.5 27.6 %collective-permute-done = f32[4,3,88,176]{3,2,1,0:T(8,128)S(1)} collective-permute-done((f32[4,3,88,176]{3,2,1,0:T(8,128)}, f32[4,3,88,176]{3,2,1,0:T(8,128)S(1)}, u32[]{:S(2)}, u32[]{:S(2)}) %collective-permute-start) | collective-permute-done | bytes 743456 | tf_op jit(solution)/shard_map/while/body/eval_jaxpr/ppermute | solution.py:41
  389.0 26.7 %collective-permute-done = f32[4,3,88,176]{3,2,1,0:T(8,128)S(1)} collective-permute-done((f32[4,3,88,176]{3,2,1,0:T(8,128)}, f32[4,3,88,176]{3,2,1,0:T(8,128)S(1)}, u32[]{:S(2)}, u32[]{:S(2)}) %collective-permute-start) | collective-permute-done | bytes 743456 | tf_op jit(solution)/shard_map/while/body/eval_jaxpr/ppermute | solution.py:41
  424.6 25.8 %collective-permute-done = f32[4,3,88,176]{3,2,1,0:T(8,128)S(1)} collective-permute-done((f32[4,3,88,176]{3,2,1,0:T(8,128)}, f32[4,3,88,176]{3,2,1,0:T(8,128)S(1)}, u32[]{:S(2)}, u32[]{:S(2)}) %collective-permute-start) | collective-permute-done | bytes 743456 | tf_op jit(solution)/shard_map/while/body/eval_jaxpr/ppermute | solution.py:41
  459.3 24.9 %collective-permute-done = f32[4,3,88,176]{3,2,1,0:T(8,128)S(1)} collective-permute-done((f32[4,3,88,176]{3,2,1,0:T(8,128)}, f32[4,3,88,176]{3,2,1,0:T(8,128)S(1)}, u32[]{:S(2)}, u32[]{:S(2)}) %collective-permute-start) | collective-permute-done | bytes 743456 | tf_op jit(solution)/shard_map/while/body/eval_jaxpr/ppermute | solution.py:41
  493.1 24.0 %collective-permute-done = f32[4,3,88,176]{3,2,1,0:T(8,128)S(1)} collective-permute-done((f32[4,3,88,176]{3,2,1,0:T(8,128)}, f32[4,3,88,176]{3,2,1,0:T(8,128)S(1)}, u32[]{:S(2)}, u32[]{:S(2)}) %collective-permute-start) | collective-permute-done | bytes 743456 | tf_op jit(solution)/shard_map/while/body/eval_jaxpr/ppermute | solution.py:41
  525.9 23.0 %collective-permute-done = f32[4,3,88,176]{3,2,1,0:T(8,128)S(1)} collective-permute-done((f32[4,3,88,176]{3,2,1,0:T(8,128)}, f32[4,3,88,176]{3,2,1,0:T(8,128)S(1)}, u32[]{:S(2)}, u32[]{:S(2)}) %collective-permute-start) | collective-permute-done | bytes 743456 | tf_op jit(solution)/shard_map/while/body/eval_jaxpr/ppermute | solution.py:41
  561.8 5.2 convolution_bitcast_fusion.1
  570.4 5.0 reshape.1391
  575.4 28.7 %all_to_all.90 = f32[16,1,24576]{2,1,0:T(1,128)S(1)} all-to-all(f32[16,1,24576]{2,1,0:T(1,128)S(1)} %reshape.1391), channel_id=1, replica_groups=mesh['tm'=8,'py'=4,'pz'=4] {'py','pz'}, dimensions={0} | all-to-all | bytes 3145728 | tf_op jit(solution)/shard_map/all_to_all | solution.py:222
  604.1 4.4 reduce.9
  608.5 4.0 reshape.1392
  616.0 13.4 %fusion.115 = f32[1,4,32,32,128]{4,3,2,1,0:T(8,128)} fusion(f32[4,2,48,32,32]{4,3,2,1,0:T(8,128)S(1)} %bitcast.367, f32[48]{0:T(128)S(1)} %copy-done.33, f32[1,48,128]{2,1,0:T(8,128)S(1)} %copy-done.22, f32[1,48,128]{2,1,0:T(8,128)S(1)} %copy-done.24), kind=kOutput, calls=%fused_computation.129 | convolution fusion | flops 604004352 | bytes 3719360 | tf_op jit(solution)/shard_map/ofcayz,cax->fyzx/dot_general | solution.py:45
  (415 shorter events, 133.2 us)
Async XLA Ops:
  0.0 1.6 copy-start
  0.1 203.1 %copy-start.21 = (f32[1,48,128]{2,1,0:T(8,128)}, f32[1,48,128]{2,1,0:T(8,128)S(1)}, u32[]{:S(2)}) copy-start(f32[1,48,128]{2,1,0:T(8,128)S(1)} %get-tuple-element.391) | copy-start | bytes 73732
  0.1 203.1 %copy-start.23 = (f32[1,48,128]{2,1,0:T(8,128)}, f32[1,48,128]{2,1,0:T(8,128)S(1)}, u32[]{:S(2)}) copy-start(f32[1,48,128]{2,1,0:T(8,128)S(1)} %get-tuple-element.392) | copy-start | bytes 73732
  14.1 21.4 %all-to-all-start.1 = ((f32[16,1,12288]{2,1,0:T(1,128)}), f32[16,1,12288]{2,1,0:T(1,128)}, u32[]{:S(2)}, u32[]{:S(2)}) async-start(f32[16,1,12288]{2,1,0:T(1,128)} %reshape.1381), calls=%async_computation.1 | async-start | bytes 1572864 | tf_op jit(solution)/shard_map/all_to_all | solution.py:30
  35.6 21.4 %all-to-all-start = ((f32[16,1,12288]{2,1,0:T(1,128)}), f32[16,1,12288]{2,1,0:T(1,128)}, u32[]{:S(2)}, u32[]{:S(2)}) async-start(f32[16,1,12288]{2,1,0:T(1,128)} %reshape.1383), calls=%async_computation | async-start | bytes 1572864 | tf_op jit(solution)/shard_map/all_to_all | solution.py:30
  41.0 37.0 %copy-start.17 = (f32[1,88,2,128]{3,1,0,2:T(8,128)}, f32[1,88,2,128]{3,1,0,2:T(8,128)S(1)}, u32[]{:S(2)}) copy-start(f32[1,88,2,128]{3,1,0,2:T(8,128)S(1)} %get-tuple-element.376) | copy-start | bytes 270340
  69.5 1.4 copy-start.2
  72.0 0.7 copy-start.3
  72.2 0.7 copy-start.5
  72.3 0.7 copy-start.7
  75.1 2.9 copy-start.19
  81.4 2.3 copy-start.25
  81.4 2.3 copy-start.27
  81.4 2.3 copy-start.29
  110.2 43.6 %all-to-all-start.2 = ((f32[16,1,43008]{2,1,0:T(1,128)}), f32[16,1,43008]{2,1,0:T(1,128)S(1)}, u32[]{:S(2)}, u32[]{:S(2)}) async-start(f32[16,1,43008]{2,1,0:T(1,128)} %reshape.1385), calls=%async_computation.2 | async-start | bytes 5505024 | tf_op jit(solution)/shard_map/all_to_all | solution.py:222
  117.5 63.3 %copy-start.32 = (f32[48]{0:T(128)}, f32[48]{0:T(128)S(1)}, u32[]{:S(2)}) copy-start(f32[48]{0:T(128)S(1)} %fusion.265) | copy-start | bytes 580
  223.1 26.7 %all-to-all-start.3 = ((f32[16,1,18432]{2,1,0:T(1,128)}), f32[16,1,18432]{2,1,0:T(1,128)}, u32[]{:S(2)}, u32[]{:S(2)}) async-start(f32[16,1,18432]{2,1,0:T(1,128)} %reshape.1389), calls=%async_computation.3 | async-start | bytes 2359296 | tf_op jit(solution)/shard_map/all_to_all | solution.py:30
  240.5 13.9 %copy-start.16 = (f32[1,3,88,2,88]{4,2,3,1,0:T(8,128)S(1)}, f32[1,3,88,2,88]{4,2,3,1,0:T(8,128)}, u32[]{:S(2)}) copy-start(f32[1,3,88,2,88]{4,2,3,1,0:T(8,128)} %get-tuple-element.364) | copy-start | bytes 557572
  249.8 29.6 %all-to-all-start.4 = ((f32[16,1,18432]{2,1,0:T(1,128)}), f32[16,1,18432]{2,1,0:T(1,128)S(1)}, u32[]{:S(2)}, u32[]{:S(2)}) async-start(f32[16,1,18432]{2,1,0:T(1,128)} %reshape.1387), calls=%async_computation.4 | async-start | bytes 2359296 | tf_op jit(solution)/shard_map/all_to_all | solution.py:30
  301.4 1.0 copy-start.4
  301.5 1.0 copy-start.6
  301.5 1.1 copy-start.8
  303.5 6.1 copy-start.9
  303.5 6.1 copy-start.11
  303.8 5.8 copy-start.13
  309.4 1.0 copy-start.15
  312.3 31.2 %collective-permute-start = (f32[4,3,88,176]{3,2,1,0:T(8,128)}, f32[4,3,88,176]{3,2,1,0:T(8,128)S(1)}, u32[]{:S(2)}, u32[]{:S(2)}) collective-permute-start(f32[4,3,88,176]{3,2,1,0:T(8,128)} %get-tuple-element.534), channel_id=1, source_target_pairs={{0,16},{16,32},{32,48},{48,64},{64,80},{80,96},{96,112},{1,17},{17... | collective-permute-start | bytes 2230280 | tf_op jit(solution)/shard_map/while/body/eval_jaxpr/ppermute | solution.py:41
  350.3 29.8 %collective-permute-start = (f32[4,3,88,176]{3,2,1,0:T(8,128)}, f32[4,3,88,176]{3,2,1,0:T(8,128)S(1)}, u32[]{:S(2)}, u32[]{:S(2)}) collective-permute-start(f32[4,3,88,176]{3,2,1,0:T(8,128)} %get-tuple-element.534), channel_id=1, source_target_pairs={{0,16},{16,32},{32,48},{48,64},{64,80},{80,96},{96,112},{1,17},{17... | collective-permute-start | bytes 2230280 | tf_op jit(solution)/shard_map/while/body/eval_jaxpr/ppermute | solution.py:41
  386.8 28.9 %collective-permute-start = (f32[4,3,88,176]{3,2,1,0:T(8,128)}, f32[4,3,88,176]{3,2,1,0:T(8,128)S(1)}, u32[]{:S(2)}, u32[]{:S(2)}) collective-permute-start(f32[4,3,88,176]{3,2,1,0:T(8,128)} %get-tuple-element.534), channel_id=1, source_target_pairs={{0,16},{16,32},{32,48},{48,64},{64,80},{80,96},{96,112},{1,17},{17... | collective-permute-start | bytes 2230280 | tf_op jit(solution)/shard_map/while/body/eval_jaxpr/ppermute | solution.py:41
  422.4 28.0 %collective-permute-start = (f32[4,3,88,176]{3,2,1,0:T(8,128)}, f32[4,3,88,176]{3,2,1,0:T(8,128)S(1)}, u32[]{:S(2)}, u32[]{:S(2)}) collective-permute-start(f32[4,3,88,176]{3,2,1,0:T(8,128)} %get-tuple-element.534), channel_id=1, source_target_pairs={{0,16},{16,32},{32,48},{48,64},{64,80},{80,96},{96,112},{1,17},{17... | collective-permute-start | bytes 2230280 | tf_op jit(solution)/shard_map/while/body/eval_jaxpr/ppermute | solution.py:41
  457.1 27.0 %collective-permute-start = (f32[4,3,88,176]{3,2,1,0:T(8,128)}, f32[4,3,88,176]{3,2,1,0:T(8,128)S(1)}, u32[]{:S(2)}, u32[]{:S(2)}) collective-permute-start(f32[4,3,88,176]{3,2,1,0:T(8,128)} %get-tuple-element.534), channel_id=1, source_target_pairs={{0,16},{16,32},{32,48},{48,64},{64,80},{80,96},{96,112},{1,17},{17... | collective-permute-start | bytes 2230280 | tf_op jit(solution)/shard_map/while/body/eval_jaxpr/ppermute | solution.py:41
  490.9 26.1 %collective-permute-start = (f32[4,3,88,176]{3,2,1,0:T(8,128)}, f32[4,3,88,176]{3,2,1,0:T(8,128)S(1)}, u32[]{:S(2)}, u32[]{:S(2)}) collective-permute-start(f32[4,3,88,176]{3,2,1,0:T(8,128)} %get-tuple-element.534), channel_id=1, source_target_pairs={{0,16},{16,32},{32,48},{48,64},{64,80},{80,96},{96,112},{1,17},{17... | collective-permute-start | bytes 2230280 | tf_op jit(solution)/shard_map/while/body/eval_jaxpr/ppermute | solution.py:41
  523.8 25.2 %collective-permute-start = (f32[4,3,88,176]{3,2,1,0:T(8,128)}, f32[4,3,88,176]{3,2,1,0:T(8,128)S(1)}, u32[]{:S(2)}, u32[]{:S(2)}) collective-permute-start(f32[4,3,88,176]{3,2,1,0:T(8,128)} %get-tuple-element.534), channel_id=1, source_target_pairs={{0,16},{16,32},{32,48},{48,64},{64,80},{80,96},{96,112},{1,17},{17... | collective-permute-start | bytes 2230280 | tf_op jit(solution)/shard_map/while/body/eval_jaxpr/ppermute | solution.py:41
  555.8 1.8 copy-start.10
  555.9 1.8 copy-start.12
  555.9 1.8 copy-start.14
  555.9 1.8 copy-start.31
  557.7 0.9 copy-start.18
  557.7 0.9 copy-start.20
  560.9 0.8 copy-start.26
  560.9 0.9 copy-start.28
  560.9 0.9 copy-start.30
  612.5 3.5 copy-start.22
  612.5 3.5 copy-start.24
  612.5 3.5 copy-start.33
  616.0 13.4 %copy-start.1 = (f32[1,4,32,32,128]{4,3,2,1,0:T(8,128)S(1)}, f32[1,4,32,32,128]{4,3,2,1,0:T(8,128)}, u32[]{:S(2)}) copy-start(f32[1,4,32,32,128]{4,3,2,1,0:T(8,128)} %param.3) | copy-start | bytes 6291460
where the time goes:
time: 639 us; the launch traced here: 630 us
  waiting for transfers between devices  233 us (36%)
  local copies, waits for them, and re-layouts  125 us (20%)
  matrix products  99.3 us (16%)
  other arithmetic  96.8 us (15%)
  starting transfers between devices  44.2 us (7%)
  blocking collectives  28.7 us (4%)
    ppermute x7, waiting for transfers between devices, passed_along(): return lax.ppermute(value, axis, pairs)  179 us
    dot_general x16, matrix products, product(): jnp.einsum(form, left, right, precision=lax.Precision.HIGHEST, preferred_...  99.3 us
    unnamed x85, local copies, waits for them, and re-layouts  65.6 us
    all_to_all x1, waiting for transfers between devices, to_grid(): lax.all_to_all(blocks, ('py', 'pz'), split_axis=0, concat_axis=3, tiled=T...  36.2 us
    all_to_all x1, blocking collectives, to_grid(): lax.all_to_all(blocks, ('py', 'pz'), split_axis=0, concat_axis=3, tiled=T...  28.7 us
    slice x6, local copies, waits for them, and re-layouts, items_in_groups(): lax.slice_in_dim(a, k * (items // count), (k + 1) * (items // count), axi...  24.7 us
    all_to_all x4, starting transfers between devices, items_in_groups(): lax.all_to_all(group, axis, split_axis=split_dim, concat_axis=concat_dim,...  21.7 us
    all_to_all x4, other arithmetic, items_in_groups(): lax.all_to_all(group, axis, split_axis=split_dim, concat_axis=concat_dim,...  19.5 us
  transfers between devices with their start and end apart: 12, of which 10 were waited for; matrix products, arithmetic and copies ran while one was open for 10% of the time, Pallas kernels for 0%

commit v1 on v0

v1 whole, which is shorter than its diff:
```python
import functools

import jax
import jax.numpy as jnp
import numpy as np
from jax import lax
from jax.experimental import pallas as pl
from jax.experimental.pallas import tpu as pltpu
from jax.sharding import PartitionSpec as P

KMAX = 42
KCO = 21
N = 128
KY = 96
PLANES = 3
GROUP = 16
BLOCK = 32
MODE_ROWS = 2 * PLANES * GROUP
SCAN = 6
MESH = pl.DeviceIdType.MESH
VMEM_BYTES = 50 << 20

time_step = 0.01
coriolis = 6.0
buoyancy_square = 100.0
viscosity = 0.001
diffusivity = 0.001


def halves(table):
    exact = jnp.asarray(table, jnp.float32)
    high = exact.astype(jnp.bfloat16)
    low = (exact - high.astype(jnp.float32)).astype(jnp.bfloat16)
    return high, low


def tables():
    scale = N**-0.5
    cells = np.arange(N)
    waves_x = np.arange(GROUP)[:, None] + GROUP * np.arange(PLANES)[None, :]
    angle = 2 * np.pi / N * ((waves_x[:, :, None] * cells) % N)
    inside = (waves_x <= KMAX)[:, :, None] * scale
    fore = np.stack([np.cos(angle), -np.sin(angle)], axis=2) * inside[:, :, None]
    weight = np.where(waves_x == 0, 1.0, 2.0)[:, :, None, None]
    back = fore * weight
    rest = ((0, N - MODE_ROWS), (0, 0))
    fore = np.pad(fore.reshape(MODE_ROWS, N), rest).T
    back = np.pad(back.reshape(MODE_ROWS, N), rest)

    def one_pass(table):
        high, low = halves(table)
        return jnp.concatenate(
            [
                jnp.concatenate([high, low], axis=1),
                jnp.concatenate([high, jnp.zeros_like(high)], axis=1),
            ]
        )

    def pair(slots):
        waves = np.arange(slots) - KMAX
        angle = 2 * np.pi / N * ((waves[:, None] * cells[None, :]) % N)
        inside = (waves <= KMAX)[:, None] * scale
        return np.cos(angle) * inside, np.sin(angle) * inside

    cos_y, sin_y = pair(KY)
    cos_z, sin_z = pair(N)
    fore_y = np.block([[cos_y, sin_y], [-sin_y, cos_y]])
    back_y = np.block([[cos_y.T, -sin_y.T], [sin_y.T, cos_y.T]])
    fore_z = np.block([[cos_z.T, -sin_z.T], [sin_z.T, cos_z.T]])
    back_z = np.block([[cos_z, sin_z], [-sin_z, cos_z]])
    stack = lambda table: jnp.concatenate(halves(table))
    return dict(
        fore_x=one_pass(fore),
        back_x=one_pass(back),
        fore_y=stack(fore_y),
        back_y=stack(back_y),
        fore_z=stack(fore_z),
        back_z=stack(back_z),
    )


def split(values):
    high = values.astype(jnp.bfloat16)
    low = (values - high.astype(jnp.float32)).astype(jnp.bfloat16)
    return high, low


def mul(left, right):
    return jnp.dot(left, right, preferred_element_type=jnp.float32)


def by_x(values, table):
    out = mul(jnp.concatenate(split(values), axis=1), table[...])
    return out[:, :N] + out[:, N:]


def by_left(table, values):
    rows = table.shape[0] // 2
    high, low = split(values)
    out = mul(table[...], high)
    return out[:rows] + out[rows:] + mul(table[:rows], low)


def by_right(values, table):
    rows = table.shape[0] // 2
    high, low = split(values)
    return mul(high, table[:rows]) + mul(low, table[:rows]) + mul(high, table[rows:])


def swap_groups(parts):
    lane = lax.broadcasted_iota(jnp.int32, parts[0].shape, 1)
    low_half = lane < 64
    even = (lane // 32) % 2 == 0
    a0, a1, a2, a3 = parts
    p0 = jnp.where(low_half, a0, pltpu.roll(a2, 64, 1))
    p2 = jnp.where(low_half, pltpu.roll(a0, 64, 1), a2)
    p1 = jnp.where(low_half, a1, pltpu.roll(a3, 64, 1))
    p3 = jnp.where(low_half, pltpu.roll(a1, 64, 1), a3)
    return (
        jnp.where(even, p0, pltpu.roll(p1, 32, 1)),
        jnp.where(even, pltpu.roll(p0, 96, 1), p1),
        jnp.where(even, p2, pltpu.roll(p3, 32, 1)),
        jnp.where(even, pltpu.roll(p2, 96, 1), p3),
    )


def place():
    tm, py, pz = lax.axis_index("tm"), lax.axis_index("py"), lax.axis_index("pz")
    return tm, py, pz, py * 4 + pz


def meet_group(barrier):
    tm, py, pz, _ = place()

    def greet(i, carry):
        peer = (tm, (py + i // 4) % 4, (pz + i % 4) % 4)
        pl.semaphore_signal(barrier, inc=1, device_id=peer, device_id_type=MESH)
        return carry

    lax.fori_loop(1, GROUP, greet, 0)


def chunk(owner, plane):
    rows = 2 * BLOCK
    start = pl.multiple_of((owner * PLANES + plane) * rows, rows)
    return pl.ds(start, rows)


class Exchange:
    def __init__(self, source, target, send, receive, own):
        self.source, self.target = source, target
        self.send, self.receive, self.own = send, receive, own

    def local(self, plane):
        _, _, _, me = place()
        part = chunk(me, plane)
        return pltpu.make_async_copy(
            self.source.at[part, :], self.target.at[part, :], self.own.at[plane]
        )

    def remote(self, i, plane, origin):
        tm, py, pz, me = place()
        to_y, to_z = (py + i // 4) % 4, (pz + i % 4) % 4
        from_y, from_z = (py + 4 - i // 4) % 4, (pz + 4 - i % 4) % 4
        where = (from_y * 4 + from_z) if origin else me
        index = plane * GROUP + i
        return pltpu.make_async_remote_copy(
            src_ref=self.source.at[chunk(to_y * 4 + to_z, plane), :],
            dst_ref=self.target.at[chunk(where, plane), :],
            send_sem=self.send.at[index],
            recv_sem=self.receive.at[index],
            device_id=(tm, to_y, to_z),
            device_id_type=MESH,
        )

    def start(self, plane):
        def go(i, carry):
            self.remote(i, plane, False).start()
            return carry

        lax.fori_loop(1, GROUP, go, 0)
        self.local(plane).start()

    def arrived(self, plane):
        def go(i, carry):
            self.remote(i, plane, True).wait_recv()
            return carry

        lax.fori_loop(1, GROUP, go, 0)
        self.local(plane).wait()

    def sent(self, plane):
        def go(i, carry):
            self.remote(i, plane, False).wait_send()
            return carry

        lax.fori_loop(1, GROUP, go, 0)


def exchange_scratch():
    return [
        pltpu.VMEM((MODE_ROWS * BLOCK, N), jnp.float32),
        pltpu.VMEM((MODE_ROWS * BLOCK, N), jnp.float32),
        pltpu.SemaphoreType.DMA((PLANES * GROUP,)),
        pltpu.SemaphoreType.DMA((PLANES * GROUP,)),
        pltpu.SemaphoreType.DMA((PLANES,)),
    ]


def store_modes_x(fields, table, target, first, count):
    modes = by_x(fields, table)
    for y in range(count):
        turned = modes[y * N : (y + 1) * N].T
        target[pl.ds(first + y, MODE_ROWS, stride=BLOCK), :] = turned[:MODE_ROWS]


def load_fields_x(source, table, first, count):
    lines = []
    for y in range(count):
        rows = source[pl.ds(first + y, MODE_ROWS, stride=BLOCK), :]
        rows = jnp.concatenate([rows, jnp.zeros((N - MODE_ROWS, N), jnp.float32)])
        lines.append(rows.T)
    return by_x(jnp.concatenate(lines), table)


def fore_plane(received, plane, planes, fore_y, fore_z):
    for part in range(2):
        for block in range(4):
            blocks = []
            for s in range(4):
                start = (((block * 4 + s) * PLANES + plane) * 2 + part) * BLOCK
                blocks.append(received[pl.ds(pl.multiple_of(start, BLOCK), BLOCK), :])
            for f, piece in enumerate(swap_groups(blocks)):
                rows = pl.ds(part * N + block * BLOCK, BLOCK)
                planes[f // 2, rows, (f % 2) * N : (f % 2 + 1) * N] = piece
    lines = []
    for duo in range(2):
        along_y = by_left(fore_y, planes[duo])
        for f in range(2):
            own = along_y[:, f * N : (f + 1) * N]
            lines.append(jnp.concatenate([own[:KY], own[KY:]], axis=1))
    return by_right(jnp.concatenate(lines), fore_z)


def back_plane(modes, plane, target, back_y, back_z):
    along_z = by_right(modes, back_z)
    fields = []
    for duo in range(2):
        both = []
        for f in range(2):
            own = along_z[(2 * duo + f) * KY : (2 * duo + f + 1) * KY]
            both.append(jnp.concatenate([own[:, :N], own[:, N:]]))
        along_y = by_left(back_y, jnp.concatenate(both, axis=1))
        fields += [along_y[:, :N], along_y[:, N:]]
    for part in range(2):
        for block in range(4):
            rows = slice(part * N + block * BLOCK, part * N + (block + 1) * BLOCK)
            for s, piece in enumerate(swap_groups([field[rows] for field in fields])):
                start = (((block * 4 + s) * PLANES + plane) * 2 + part) * BLOCK
                target[pl.ds(pl.multiple_of(start, BLOCK), BLOCK), :] = piece


def waves_at(plane):
    _, _, _, me = place()
    wave_x = (me + GROUP * plane).astype(jnp.float32)
    wave_y = (lax.broadcasted_iota(jnp.int32, (KY, N), 0) - KMAX).astype(jnp.float32)
    wave_z = (lax.broadcasted_iota(jnp.int32, (KY, N), 1) - KMAX).astype(jnp.float32)
    return wave_x, wave_y, wave_z


def squared(waves):
    wave_x, wave_y, wave_z = waves
    return wave_x * wave_x + wave_y * wave_y + wave_z * wave_z


def project(velocity, waves, inverse):
    wave_x, wave_y, wave_z = waves
    along = (wave_x * velocity[0] + wave_y * velocity[1] + wave_z * velocity[2]) * inverse
    return (
        velocity[0] - wave_x * along,
        velocity[1] - wave_y * along,
        velocity[2] - wave_z * along,
    )


def linear(state, waves, square, inverse):
    pushed = project((coriolis * state[1], -coriolis * state[0], state[3]), waves, inverse)
    return (
        pushed[0] - viscosity * square * state[0],
        pushed[1] - viscosity * square * state[1],
        pushed[2] - viscosity * square * state[2],
        -buoyancy_square * state[2] - diffusivity * square * state[3],
    )


def propagate(state, waves):
    square = squared(waves)
    inverse = 1.0 / jnp.maximum(square, 1.0)
    for half_step in range(2):
        anchor = state
        for order in (4.0, 3.0, 2.0, 1.0):
            rate = linear(state, waves, square, inverse)
            state = tuple(a + (0.5 * time_step / order) * r for a, r in zip(anchor, rate))
    return state


def analysis_kernel(
    fields, fore_x, fore_y, fore_z, start, out, into, send, receive, own, planes
):
    barrier = pltpu.get_barrier_semaphore()
    meet_group(barrier)

    def lines(step, carry):
        first = step * 4
        block = fields[:, pl.ds(first, 4)]
        rows = [block[f, y] for y in range(4) for f in range(4)]
        store_modes_x(jnp.concatenate(rows), fore_x, out, first, 4)
        return carry

    lax.fori_loop(0, BLOCK // 4, lines, 0)
    pl.semaphore_wait(barrier, GROUP - 1)
    exchange = Exchange(out, into, send, receive, own)
    for plane in range(PLANES):
        exchange.start(plane)

    def finish(plane, carry):
        exchange.arrived(plane)
        modes = fore_plane(into, plane, planes, fore_y, fore_z)
        waves = waves_at(plane)
        inverse = 1.0 / jnp.maximum(squared(waves), 1.0)
        for part in range(2):
            own_lanes = slice(part * N, (part + 1) * N)
            state = [modes[f * KY : (f + 1) * KY, own_lanes] for f in range(4)]
            for f, value in enumerate(project(state[:3], waves, inverse) + (state[3],)):
                start[plane, pl.ds(f * KY, KY), own_lanes] = value
        exchange.sent(plane)
        return carry

    lax.fori_loop(0, PLANES, finish, 0)


def rate_kernel(
    start, fore_x, back_x, fore_y, back_y, fore_z, back_z, fine,
    out0, into0, send0, receive0, own0,
    out1, into1, send1, receive1, own1,
    out2, into2, send2, receive2, own2,
    planes, first_modes, second_modes,
):
    barrier = pltpu.get_barrier_semaphore()
    meet_group(barrier)
    to_grid = Exchange(out0, into0, send0, receive0, own0)
    to_modes = (
        Exchange(out1, into1, send1, receive1, own1),
        Exchange(out2, into2, send2, receive2, own2),
    )
    back_plane(start[0], 0, out0, back_y, back_z)
    pl.semaphore_wait(barrier, GROUP - 1)
    to_grid.start(0)

    def spread(plane, carry):
        back_plane(start[plane], plane, out0, back_y, back_z)
        to_grid.start(plane)
        return carry

    lax.fori_loop(1, PLANES, spread, 0)

    def gather(plane, carry):
        to_grid.arrived(plane)
        return carry

    lax.fori_loop(0, PLANES, gather, 0)

    def lines(step, carry):
        first = step * 4
        grid = load_fields_x(into0, back_x, first, 4)
        one, two = [], []
        for y in range(4):
            u, v, w, b = (
                grid[y * N + f * BLOCK : y * N + (f + 1) * BLOCK] for f in range(4)
            )
            rest = w * w
            one += [u * u - rest, v * v - rest, u * v, u * w]
            two += [v * w, u * b, v * b, w * b]
        store_modes_x(jnp.concatenate(one), fore_x, out1, first, 4)
        store_modes_x(jnp.concatenate(two), fore_x, out2, first, 4)
        return carry

    lax.fori_loop(0, BLOCK // 4, lines, 0)
    for plane in range(PLANES):
        for exchange in to_modes:
            exchange.start(plane)

    def finish(plane, carry):
        to_modes[0].arrived(plane)
        first_modes[...] = fore_plane(into1, plane, planes, fore_y, fore_z)
        to_modes[1].arrived(plane)
        second_modes[...] = fore_plane(into2, plane, planes, fore_y, fore_z)
        waves = waves_at(plane)
        wave_x, wave_y, wave_z = waves
        square = squared(waves)
        inverse = 1.0 / jnp.maximum(square, 1.0)

        def products(lanes):
            return [first_modes[f * KY : (f + 1) * KY, lanes] for f in range(4)] + [
                second_modes[f * KY : (f + 1) * KY, lanes] for f in range(4)
            ]

        for part in range(2):
            lanes = slice(part * N, (part + 1) * N)
            other = slice((1 - part) * N, (2 - part) * N)
            sign = 1.0 if part == 0 else -1.0
            xx, yy, xy, xz, yz, bx, by, bz = products(other)
            state = [start[plane, pl.ds(f * KY, KY), lanes] for f in range(4)]
            moved = (
                sign * (wave_x * xx + wave_y * xy + wave_z * xz),
                sign * (wave_x * xy + wave_y * yy + wave_z * yz),
                sign * (wave_x * xz + wave_y * yz),
            )
            lifted = sign * (wave_x * bx + wave_y * by + wave_z * bz)
            pushed = project(
                (
                    moved[0] + coriolis * state[1],
                    moved[1] - coriolis * state[0],
                    moved[2] + state[3],
                ),
                waves,
                inverse,
            )
            rates = [pushed[f] - viscosity * square * state[f] for f in range(3)]
            rates.append(
                lifted - buoyancy_square * state[2] - diffusivity * square * state[3]
            )
            for f in range(4):
                fine[plane, pl.ds(f * KY, KY), lanes] = state[f] + time_step * rates[f]
        to_grid.sent(plane)
        for exchange in to_modes:
            exchange.sent(plane)
        return carry

    lax.fori_loop(0, PLANES, finish, 0)


FIRST_ROW = 16
COARSE_ROWS = 8 * SCAN
TILE = 8 * 4 * 2


def coarse_waves(plane, row0, rows):
    _, _, _, me = place()
    row = lax.broadcasted_iota(jnp.int32, (rows, N), 0) + row0
    lane = lax.broadcasted_iota(jnp.int32, (rows, N), 1) % 64
    wave_x = (me + GROUP * plane).astype(jnp.float32)
    wave_y = (row - KMAX).astype(jnp.float32)
    wave_z = (lane - KMAX).astype(jnp.float32)
    return wave_x, wave_y, wave_z


def coarse_inside(waves):
    wave_x, wave_y, wave_z = waves
    inside = (jnp.abs(wave_y) <= KCO) & (jnp.abs(wave_z) <= KCO)
    return inside & jnp.broadcast_to(wave_x <= KCO, inside.shape)


def packed(ref, plane, f):
    rows = pl.ds(f * KY + FIRST_ROW, COARSE_ROWS)
    lane = lax.broadcasted_iota(jnp.int32, (COARSE_ROWS, N), 1)
    real, imag = ref[plane, rows, :N], ref[plane, rows, N:]
    return jnp.where(lane < 64, real, pltpu.roll(imag, 64, 1))


def last_kernel(
    fine, start, back_x, back_y, back_z, result,
    out, into, send, receive, own, merged,
    coarse_out, coarse_in, coarse_send, coarse_receive, coarse_own,
    carry_out, carry_in, carry_send, carry_receive, carry_own,
):
    tm, py, pz, me = place()
    slices = lax.axis_size("tm")
    barrier = pltpu.get_barrier_semaphore()
    meet_group(barrier)

    def greet(i, carry):
        peer = ((tm + i) % slices, py, pz)
        pl.semaphore_signal(barrier, inc=1, device_id=peer, device_id_type=MESH)
        return carry

    lax.fori_loop(1, slices, greet, 0)

    def rows_of(index):
        return pl.ds(pl.multiple_of(index * TILE, TILE), TILE)

    def coarse_copy(i, origin):
        to = (tm + i) % slices
        where = (tm + slices - i) % slices if origin else tm
        return pltpu.make_async_remote_copy(
            src_ref=coarse_out.at[rows_of(to), :],
            dst_ref=coarse_in.at[rows_of(where), :],
            send_sem=coarse_send.at[i],
            recv_sem=coarse_receive.at[i],
            device_id=(to, py, pz),
            device_id_type=MESH,
        )

    def carry_copy(i, origin):
        to = (tm + i) % slices
        where = (tm + slices - i) % slices if origin else tm
        return pltpu.make_async_remote_copy(
            src_ref=carry_out.at[rows_of(to), :],
            dst_ref=carry_in.at[rows_of(where), :],
            send_sem=carry_send.at[i],
            recv_sem=carry_receive.at[i],
            device_id=(to, py, pz),
            device_id_type=MESH,
        )

    coarse_mine = pltpu.make_async_copy(
        coarse_out.at[rows_of(tm), :], coarse_in.at[rows_of(tm), :], coarse_own
    )
    carry_mine = pltpu.make_async_copy(
        carry_out.at[rows_of(tm), :], carry_in.at[rows_of(tm), :], carry_own
    )

    for plane in range(2):
        waves = coarse_waves(plane, FIRST_ROW, COARSE_ROWS)
        keep = coarse_inside(waves).astype(jnp.float32)
        before = [packed(start, plane, f) for f in range(4)]
        after = [packed(fine, plane, f) for f in range(4)]
        moved = propagate(tuple(before), waves)
        for f in range(4):
            here = keep * after[f] - jnp.where(tm > 0, keep * moved[f], 0.0)
            for tile in range(SCAN):
                place_at = tile * TILE + (f * 2 + plane) * 8
                coarse_out[place_at : place_at + 8, :] = here[tile * 8 : tile * 8 + 8]

    pl.semaphore_wait(barrier, GROUP - 1 + slices - 1)

    def coarse_go(i, carry):
        @pl.when((tm + i) % slices < SCAN)
        def _():
            coarse_copy(i, False).start()

        return carry

    lax.fori_loop(1, slices, coarse_go, 0)

    @pl.when(tm < SCAN)
    def _():
        coarse_mine.start()

    exchange = Exchange(out, into, send, receive, own)
    back_plane(fine[2], 2, out, back_y, back_z)
    exchange.start(2)

    @pl.when(tm < SCAN)
    def _():
        def wait(i, carry):
            coarse_copy(i, True).wait_recv()
            return carry

        lax.fori_loop(1, slices, wait, 0)
        coarse_mine.wait()
        row0 = FIRST_ROW + tm * 8
        waves = [coarse_waves(plane, row0, 8) for plane in range(2)]
        keep = [coarse_inside(w).astype(jnp.float32) for w in waves]

        def step(n, state):
            base = pl.multiple_of(n * TILE, TILE)
            new = []
            for plane in range(2):
                moved = propagate(tuple(state[plane * 4 : plane * 4 + 4]), waves[plane])
                for f in range(4):
                    rows = pl.ds(base + (f * 2 + plane) * 8, 8)
                    value = coarse_in[rows, :] + keep[plane] * moved[f]
                    carry_out[rows, :] = value
                    new.append(value)
            return tuple(new)

        lax.fori_loop(0, slices, step, tuple([jnp.zeros((8, N), jnp.float32)] * 8))

        def back(i, carry):
            carry_copy(i, False).start()
            return carry

        lax.fori_loop(1, slices, back, 0)
        carry_mine.start()

    def carry_wait(i, carry):
        @pl.when((tm + slices - i) % slices < SCAN)
        def _():
            carry_copy(i, True).wait_recv()

        return carry

    lax.fori_loop(1, slices, carry_wait, 0)

    @pl.when(tm < SCAN)
    def _():
        carry_mine.wait()

    for plane in range(2):
        waves = coarse_waves(plane, FIRST_ROW, COARSE_ROWS)
        inside = coarse_inside(waves)
        lane = lax.broadcasted_iota(jnp.int32, (COARSE_ROWS, N), 1)
        here = inside & (lane < 64)
        merged[...] = fine[plane]
        for f in range(4):
            tiles = []
            for tile in range(SCAN):
                place_at = tile * TILE + (f * 2 + plane) * 8
                tiles.append(carry_in[place_at : place_at + 8, :])
            value = jnp.concatenate(tiles)
            rows = pl.ds(f * KY + FIRST_ROW, COARSE_ROWS)
            merged[rows, :N] = jnp.where(here, value, merged[rows, :N])
            merged[rows, N:] = jnp.where(here, pltpu.roll(value, 64, 1), merged[rows, N:])
        back_plane(merged[...], plane, out, back_y, back_z)
        exchange.start(plane)

    def gather(plane, carry):
        exchange.arrived(plane)
        return carry

    lax.fori_loop(0, PLANES, gather, 0)

    def lines(step, carry):
        first = step * 4
        grid = load_fields_x(into, back_x, first, 4)
        for y in range(4):
            for f in range(4):
                at = y * N + f * BLOCK
                result[f, first + y] = grid[at : at + BLOCK]
        return carry

    lax.fori_loop(0, BLOCK // 4, lines, 0)

    def done(plane, carry):
        exchange.sent(plane)
        return carry

    lax.fori_loop(0, PLANES, done, 0)

    def coarse_done(i, carry):
        @pl.when((tm + i) % slices < SCAN)
        def _():
            coarse_copy(i, False).wait_send()

        @pl.when(tm < SCAN)
        def _():
            carry_copy(i, False).wait_send()

        return carry

    lax.fori_loop(1, slices, coarse_done, 0)

    @pl.when(tm < SCAN)
    def _():
        pass


def call(kernel, name, out, scratch, collective, *args):
    return pl.pallas_call(
        kernel,
        name=name,
        out_shape=jax.ShapeDtypeStruct(out, jnp.float32),
        in_specs=[pl.BlockSpec(memory_space=pltpu.VMEM)] * len(args),
        out_specs=pl.BlockSpec(memory_space=pltpu.VMEM),
        scratch_shapes=scratch,
        compiler_params=pltpu.CompilerParams(
            collective_id=collective, has_side_effects=True, vmem_limit_bytes=VMEM_BYTES
        ),
    )(*args)


def on_device(state_old):
    t = tables()
    slices = lax.axis_size("tm")
    modes_shape = (PLANES, 4 * KY, 2 * N)
    planes = pltpu.VMEM((2, 2 * N, 2 * N), jnp.float32)
    start = call(
        analysis_kernel,
        "analysis",
        modes_shape,
        exchange_scratch() + [planes],
        0,
        state_old[0],
        t["fore_x"],
        t["fore_y"],
        t["fore_z"],
    )
    half = pltpu.VMEM((4 * KY, 2 * N), jnp.float32)
    fine = call(
        rate_kernel,
        "rate",
        modes_shape,
        exchange_scratch() * 3 + [planes, half, half],
        1,
        start,
        t["fore_x"],
        t["back_x"],
        t["fore_y"],
        t["back_y"],
        t["fore_z"],
        t["back_z"],
    )
    passes = [
        pltpu.VMEM((slices * TILE, N), jnp.float32),
        pltpu.VMEM((slices * TILE, N), jnp.float32),
        pltpu.SemaphoreType.DMA((slices,)),
        pltpu.SemaphoreType.DMA((slices,)),
        pltpu.SemaphoreType.DMA,
    ]
    result = call(
        last_kernel,
        "last",
        state_old.shape[1:],
        exchange_scratch() + [half] + passes + passes,
        2,
        fine,
        start,
        t["back_x"],
        t["back_y"],
        t["back_z"],
    )
    return result[None]


def solution(mesh):
    return jax.shard_map(
        on_device,
        mesh=mesh,
        in_specs=(P("tm", None, "py", "pz", None),),
        out_specs=P("tm", None, "py", "pz", None),
        check_vma=False,
    )
```

time: 639 us -> 148 us (0.23)
  the two profiles are of different devices: /device:TPU:8 before, /device:TPU:1 now
where the time goes in v1:
time: 148 us; the launch traced here: 147 us
  Pallas kernels  140 us (95%)
  local copies, waits for them, and re-layouts  7.47 us (5%)
    pallas_call x3, Pallas kernels, call(): pl.pallas_call(kernel, name=name, out_shape=jax.ShapeDtypeStruct(out, jnp...  140 us
    unnamed x17, local copies, waits for them, and re-layouts  7.47 us

profile of v1, /device:TPU:1, one launch (start us, length us, event | category | flops | bytes accessed | tf_op | source)
XLA Modules:
  0.0 147.3 jit_solution(9393109850033443002)
XLA Ops:
  0.0 0.0 copy-start
  0.0 1.6 %copy-done = f32[1,4,32,32,128]{4,3,2,1,0:T(8,128)S(1)} copy-done((f32[1,4,32,32,128]{4,3,2,1,0:T(8,128)S(1)}, f32[1,4,32,32,128]{4,3,2,1,0:T(8,128)}, u32[]{:S(2)}) %copy-start) | copy-done | bytes 2097176
  1.6 0.0 copy-start.3
  1.6 0.9 copy-done.3
  2.5 0.0 copy-start.5
  2.5 0.9 copy-done.5
  3.5 0.0 copy-start.7
  3.5 0.9 copy-done.7
  4.4 0.0 copy-start.1
  4.4 0.0 copy-start.2
  4.4 0.0 copy-start.4
  4.4 0.0 copy-start.6
  4.4 29.9 %analysis.1.start = f32[3,384,256]{2,1,0:T(8,128)S(1)} custom-call(f32[4,32,32,128]{3,2,1,0:T(8,128)S(1)} %bitcast.2, bf16[256,256]{1,0:T(8,128)(2,1)S(1)} %copy-done.7, bf16[384,256]{1,0:T(8,128)(2,1)S(1)} %copy-done.5, bf16[512,256]{1,0:T(8,128)(2,1)S(1)} %copy-done.3), custom_call_target="tpu_custom_call" | custom-call | tf_op jit(solution)/shard_map/analysis/pallas_call | solution.py:660
  34.3 0.0 copy-done.1
  34.3 0.0 copy-done.2
  34.3 0.0 copy-done.4
  34.3 0.0 copy-done.6
  34.3 71.6 %rate.1.fine = f32[3,384,256]{2,1,0:T(8,128)S(1)} custom-call(f32[3,384,256]{2,1,0:T(8,128)S(1)} %analysis.1.start, bf16[256,256]{1,0:T(8,128)(2,1)S(1)} %copy-done.7, bf16[256,256]{1,0:T(8,128)(2,1)S(1)} %copy-done.6, bf16[384,256]{1,0:T(8,128)(2,1)S(1)} %copy-done.5, bf16[512,192]{1,0:T(8,128)(2,1)S(1)} %copy-done.2, bf16[512,256]{1,0:T(8,128)(2,1)S(1)} %copy-done.4, ...), custom_call_target="tpu_custom_call" | custom-call | tf_op jit(solution)/shard_map/rate/pallas_call | solution.py:660
  106.0 38.2 %last.1 = f32[4,32,32,128]{3,2,1,0:T(8,128)} custom-call(f32[3,384,256]{2,1,0:T(8,128)S(1)} %rate.1.fine, f32[3,384,256]{2,1,0:T(8,128)S(1)} %analysis.1.start, bf16[256,256]{1,0:T(8,128)(2,1)S(1)} %copy-done.6, bf16[512,192]{1,0:T(8,128)(2,1)S(1)} %copy-done.2, bf16[512,256]{1,0:T(8,128)(2,1)S(1)} %copy-done.1), custom_call_target="tpu_custom_call" | custom-call | tf_op jit(solution)/shard_map/last/pallas_call | solution.py:660
  144.2 3.1 %copy.9 = f32[1,4,32,32,128]{4,3,2,1,0:T(8,128)} copy(f32[1,4,32,32,128]{4,3,2,1,0:T(8,128)} %bitcast.3) | data formatting | bytes 4194304
Async XLA Ops:
  0.0 1.6 %copy-start = (f32[1,4,32,32,128]{4,3,2,1,0:T(8,128)S(1)}, f32[1,4,32,32,128]{4,3,2,1,0:T(8,128)}, u32[]{:S(2)}) copy-start(f32[1,4,32,32,128]{4,3,2,1,0:T(8,128)} %param.7) | copy-start | bytes 6291460
  1.6 0.9 copy-start.3
  2.5 0.9 copy-start.5
  3.5 0.9 copy-start.7
  4.4 29.9 %copy-start.1 = (bf16[512,256]{1,0:T(8,128)(2,1)S(1)}, bf16[512,256]{1,0:T(8,128)(2,1)}, u32[]{:S(2)}) copy-start(bf16[512,256]{1,0:T(8,128)(2,1)} %constant.58.back_z) | copy-start | bytes 786436
  4.4 29.9 %copy-start.2 = (bf16[512,192]{1,0:T(8,128)(2,1)S(1)}, bf16[512,192]{1,0:T(8,128)(2,1)}, u32[]{:S(2)}) copy-start(bf16[512,192]{1,0:T(8,128)(2,1)} %constant.53.back_y) | copy-start | bytes 589828
  4.4 29.9 %copy-start.4 = (bf16[512,256]{1,0:T(8,128)(2,1)S(1)}, bf16[512,256]{1,0:T(8,128)(2,1)}, u32[]{:S(2)}) copy-start(bf16[512,256]{1,0:T(8,128)(2,1)} %constant.41.fore_z) | copy-start | bytes 786436
  4.4 29.9 %copy-start.6 = (bf16[256,256]{1,0:T(8,128)(2,1)S(1)}, bf16[256,256]{1,0:T(8,128)(2,1)}, u32[]{:S(2)}) copy-start(bf16[256,256]{1,0:T(8,128)(2,1)} %constant.48.back_x) | copy-start | bytes 393220

commit v2 on v1

v2 whole, which is shorter than its diff:
```python
import functools

import jax
import jax.numpy as jnp
import numpy as np
from jax import lax
from jax.experimental import pallas as pl
from jax.experimental.pallas import tpu as pltpu
from jax.sharding import PartitionSpec as P

KMAX = 42
KCO = 21
N = 128
KY = 96
PLANES = 3
GROUP = 16
BLOCK = 32
MODE_ROWS = 88
HOLDERS = KMAX + 1 - 2 * GROUP
GRID_ROWS = MODE_ROWS * BLOCK
PLANE_ROWS = PLANES * GROUP * 2 * BLOCK
SCAN = 6
MESH = pl.DeviceIdType.MESH
VMEM_BYTES = 50 << 20

time_step = 0.01
coriolis = 6.0
buoyancy_square = 100.0
viscosity = 0.001
diffusivity = 0.001


def halves(table):
    exact = np.asarray(table, np.float32)
    high = exact.astype(jnp.bfloat16)
    low = (exact - high.astype(np.float32)).astype(jnp.bfloat16)
    return high, low


def tables():
    scale = N**-0.5
    cells = np.arange(N)
    waves_x = np.arange(PLANES * GROUP)
    angle = 2 * np.pi / N * ((waves_x[:, None] * cells) % N)
    inside = (waves_x <= KMAX)[:, None] * scale
    fore = np.stack([np.cos(angle), -np.sin(angle)], axis=1) * inside[:, None]
    weight = np.where(waves_x == 0, 1.0, 2.0)[:, None, None]
    back = fore * weight
    rest = ((0, N - 2 * PLANES * GROUP), (0, 0))
    fore = np.pad(fore.reshape(-1, N), rest).T
    back = np.pad(back.reshape(-1, N), rest)

    def one_pass(table):
        high, low = halves(table)
        return np.concatenate(
            [
                np.concatenate([high, low], axis=1),
                np.concatenate([high, np.zeros_like(high)], axis=1),
            ]
        )

    def pair(slots):
        waves = np.arange(slots) - KMAX
        angle = 2 * np.pi / N * ((waves[:, None] * cells[None, :]) % N)
        inside = (waves <= KMAX)[:, None] * scale
        return np.cos(angle) * inside, np.sin(angle) * inside

    cos_y, sin_y = pair(KY)
    cos_z, sin_z = pair(N)
    fore_y = np.block([[cos_y, sin_y], [-sin_y, cos_y]])
    back_y = np.block([[cos_y.T, -sin_y.T], [sin_y.T, cos_y.T]])
    fore_z = np.block([[cos_z.T, -sin_z.T], [sin_z.T, cos_z.T]])
    back_z = np.block([[cos_z, sin_z], [-sin_z, cos_z]])
    stack = lambda table: np.concatenate(halves(table))
    return (
        one_pass(fore),
        one_pass(back),
        stack(fore_y),
        stack(back_y),
        stack(fore_z),
        stack(back_z),
    )


def split(values):
    high = values.astype(jnp.bfloat16)
    low = (values - high.astype(jnp.float32)).astype(jnp.bfloat16)
    return high, low


def mul(left, right):
    return jnp.dot(left, right, preferred_element_type=jnp.float32)


def by_x(values, table):
    out = mul(jnp.concatenate(split(values), axis=1), table[...])
    return out[:, :N] + out[:, N:]


def by_left(table, values):
    rows = table.shape[0] // 2
    high, low = split(values)
    out = mul(table[...], high)
    return out[:rows] + out[rows:] + mul(table[:rows], low)


def by_right(values, table):
    rows = table.shape[0] // 2
    high, low = split(values)
    return mul(high, table[:rows]) + mul(low, table[:rows]) + mul(high, table[rows:])


def swap_groups(parts):
    lane = lax.broadcasted_iota(jnp.int32, parts[0].shape, 1)
    low_half = lane < 64
    even = (lane // 32) % 2 == 0
    a0, a1, a2, a3 = parts
    p0 = jnp.where(low_half, a0, pltpu.roll(a2, 64, 1))
    p2 = jnp.where(low_half, pltpu.roll(a0, 64, 1), a2)
    p1 = jnp.where(low_half, a1, pltpu.roll(a3, 64, 1))
    p3 = jnp.where(low_half, pltpu.roll(a1, 64, 1), a3)
    return (
        jnp.where(even, p0, pltpu.roll(p1, 32, 1)),
        jnp.where(even, pltpu.roll(p0, 96, 1), p1),
        jnp.where(even, p2, pltpu.roll(p3, 32, 1)),
        jnp.where(even, pltpu.roll(p2, 96, 1), p3),
    )


def place():
    tm, py, pz = lax.axis_index("tm"), lax.axis_index("py"), lax.axis_index("pz")
    return tm, py, pz, py * 4 + pz


def chunk(owner, plane):
    rows = 2 * BLOCK
    return pl.ds(pl.multiple_of((plane * GROUP + owner) * rows, rows), rows)


class Exchange:
    def __init__(self, refs, to_modes):
        self.source, self.target, self.send, self.receive, self.own = refs
        self.to_modes = to_modes

    def local(self, plane):
        _, _, _, me = place()
        part = chunk(me, plane)
        return pltpu.make_async_copy(
            self.source.at[part, :], self.target.at[part, :], self.own.at[plane]
        )

    def remote(self, i, plane):
        tm, py, pz, me = place()
        to_y, to_z = (py + i // 4) % 4, (pz + i % 4) % 4
        return pltpu.make_async_remote_copy(
            src_ref=self.source.at[chunk(to_y * 4 + to_z, plane), :],
            dst_ref=self.target.at[chunk(me, plane), :],
            send_sem=self.send.at[plane],
            recv_sem=self.receive.at[plane],
            device_id=(tm, to_y, to_z),
            device_id_type=MESH,
        )

    def amount(self, count, plane):
        tm, py, pz, _ = place()
        rows = pl.ds(0, count * 2 * BLOCK)
        return pltpu.make_async_remote_copy(
            src_ref=self.source.at[rows, :],
            dst_ref=self.target.at[rows, :],
            send_sem=self.send.at[plane],
            recv_sem=self.receive.at[plane],
            device_id=(tm, (py + 1) % 4, pz),
            device_id_type=MESH,
        )

    def start(self, plane):
        _, py, pz, me = place()

        def go(i, carry):
            to = (py + i // 4) % 4 * 4 + (pz + i % 4) % 4
            wanted = (to if self.to_modes else me) + GROUP * plane <= KMAX

            @pl.when(wanted)
            def _():
                self.remote(i, plane).start()

            return carry

        lax.fori_loop(1, GROUP, go, 0)

        @pl.when(me + GROUP * plane <= KMAX)
        def _():
            self.local(plane).start()

    def modes_side(self, plane, done):
        _, _, _, me = place()

        @pl.when(me + GROUP * plane <= KMAX)
        def _():
            done(self.amount(GROUP - 1, plane))

    def grid_side(self, plane, done):
        _, _, _, me = place()

        @pl.when(plane < PLANES - 1)
        def _():
            done(self.amount(GROUP - 1, plane))

        @pl.when((plane == PLANES - 1) & (me < HOLDERS))
        def _():
            done(self.amount(HOLDERS - 1, plane))

        @pl.when((plane == PLANES - 1) & (me >= HOLDERS))
        def _():
            done(self.amount(HOLDERS, plane))

    def arrived(self, plane):
        _, _, _, me = place()
        side = self.modes_side if self.to_modes else self.grid_side
        side(plane, lambda copy: copy.wait_recv())

        @pl.when(me + GROUP * plane <= KMAX)
        def _():
            self.local(plane).wait()

    def sent(self, plane):
        side = self.grid_side if self.to_modes else self.modes_side
        side(plane, lambda copy: copy.wait_send())


def exchange_scratch(to_modes):
    sizes = (GRID_ROWS, PLANE_ROWS)
    source, target = sizes if to_modes else sizes[::-1]
    return [
        pltpu.VMEM((source, N), jnp.float32),
        pltpu.VMEM((target, N), jnp.float32),
        pltpu.SemaphoreType.DMA((PLANES,)),
        pltpu.SemaphoreType.DMA((PLANES,)),
        pltpu.SemaphoreType.DMA((PLANES,)),
    ]


def store_modes_x(fields, table, target, first, count):
    modes = by_x(fields, table)
    for y in range(count):
        turned = modes[y * N : (y + 1) * N].T
        target[pl.ds(first + y, MODE_ROWS, stride=BLOCK), :] = turned[:MODE_ROWS]


def load_fields_x(source, table, first, count):
    lines = []
    for y in range(count):
        rows = source[pl.ds(first + y, MODE_ROWS, stride=BLOCK), :]
        rows = jnp.concatenate([rows, jnp.zeros((N - MODE_ROWS, N), jnp.float32)])
        lines.append(rows.T)
    return by_x(jnp.concatenate(lines), table)


def fore_plane(received, plane, planes, fore_y, fore_z):
    for part in range(2):
        for block in range(4):
            blocks = []
            for s in range(4):
                start = ((plane * GROUP + block * 4 + s) * 2 + part) * BLOCK
                blocks.append(received[pl.ds(pl.multiple_of(start, BLOCK), BLOCK), :])
            for f, piece in enumerate(swap_groups(blocks)):
                rows = pl.ds(part * N + block * BLOCK, BLOCK)
                planes[f // 2, rows, (f % 2) * N : (f % 2 + 1) * N] = piece
    lines = []
    for duo in range(2):
        along_y = by_left(fore_y, planes[duo])
        for f in range(2):
            own = along_y[:, f * N : (f + 1) * N]
            lines.append(jnp.concatenate([own[:KY], own[KY:]], axis=1))
    return by_right(jnp.concatenate(lines), fore_z)


def back_plane(modes, plane, target, back_y, back_z):
    along_z = by_right(modes, back_z)
    fields = []
    for duo in range(2):
        both = []
        for f in range(2):
            own = along_z[(2 * duo + f) * KY : (2 * duo + f + 1) * KY]
            both.append(jnp.concatenate([own[:, :N], own[:, N:]]))
        along_y = by_left(back_y, jnp.concatenate(both, axis=1))
        fields += [along_y[:, :N], along_y[:, N:]]
    for part in range(2):
        for block in range(4):
            rows = slice(part * N + block * BLOCK, part * N + (block + 1) * BLOCK)
            for s, piece in enumerate(swap_groups([field[rows] for field in fields])):
                start = ((plane * GROUP + block * 4 + s) * 2 + part) * BLOCK
                target[pl.ds(pl.multiple_of(start, BLOCK), BLOCK), :] = piece


def waves_at(plane):
    _, _, _, me = place()
    wave_x = (me + GROUP * plane).astype(jnp.float32)
    wave_y = (lax.broadcasted_iota(jnp.int32, (KY, N), 0) - KMAX).astype(jnp.float32)
    wave_z = (lax.broadcasted_iota(jnp.int32, (KY, N), 1) - KMAX).astype(jnp.float32)
    return wave_x, wave_y, wave_z


def squared(waves):
    wave_x, wave_y, wave_z = waves
    return wave_x * wave_x + wave_y * wave_y + wave_z * wave_z


def project(velocity, waves, inverse):
    wave_x, wave_y, wave_z = waves
    along = (wave_x * velocity[0] + wave_y * velocity[1] + wave_z * velocity[2]) * inverse
    return (
        velocity[0] - wave_x * along,
        velocity[1] - wave_y * along,
        velocity[2] - wave_z * along,
    )


def linear(state, waves, square, inverse):
    pushed = project((coriolis * state[1], -coriolis * state[0], state[3]), waves, inverse)
    return (
        pushed[0] - viscosity * square * state[0],
        pushed[1] - viscosity * square * state[1],
        pushed[2] - viscosity * square * state[2],
        -buoyancy_square * state[2] - diffusivity * square * state[3],
    )


def propagate(state, waves):
    square = squared(waves)
    inverse = 1.0 / jnp.maximum(square, 1.0)
    for half_step in range(2):
        anchor = state
        for order in (4.0, 3.0, 2.0, 1.0):
            rate = linear(state, waves, square, inverse)
            state = tuple(a + (0.5 * time_step / order) * r for a, r in zip(anchor, rate))
    return state


FIRST_ROW = 16
COARSE_ROWS = 8 * SCAN
TILE = 8 * 4
STEP = 4


def coarse_waves(plane, row0, rows):
    _, _, _, me = place()
    row = lax.broadcasted_iota(jnp.int32, (rows, N), 0) + row0
    lane = lax.broadcasted_iota(jnp.int32, (rows, N), 1) % 64
    wave_x = (me + GROUP * plane).astype(jnp.float32)
    wave_y = (row - KMAX).astype(jnp.float32)
    wave_z = (lane - KMAX).astype(jnp.float32)
    return wave_x, wave_y, wave_z


def coarse_inside(waves):
    wave_x, wave_y, wave_z = waves
    inside = (jnp.abs(wave_y) <= KCO) & (jnp.abs(wave_z) <= KCO)
    return inside & jnp.broadcast_to(wave_x <= KCO, inside.shape)


def packed(ref, plane, f):
    rows = pl.ds(f * KY + FIRST_ROW, COARSE_ROWS)
    lane = lax.broadcasted_iota(jnp.int32, (COARSE_ROWS, N), 1)
    real, imag = ref[plane, rows, :N], ref[plane, rows, N:]
    return jnp.where(lane < 64, real, pltpu.roll(imag, 64, 1))


class Passing:
    def __init__(self, refs):
        self.source, self.target, self.send, self.receive, self.own = refs

    def rows(self, owner, plane):
        slices = lax.axis_size("tm")
        return pl.ds(pl.multiple_of((plane * slices + owner) * TILE, TILE), TILE)

    def remote(self, i, plane, origin):
        tm, py, pz, _ = place()
        slices = lax.axis_size("tm")
        to = (tm + i) % slices
        where = (tm + slices - i) % slices if origin else tm
        return pltpu.make_async_remote_copy(
            src_ref=self.source.at[self.rows(to, plane), :],
            dst_ref=self.target.at[self.rows(where, plane), :],
            send_sem=self.send.at[plane * slices + i],
            recv_sem=self.receive.at[plane * slices + i],
            device_id=(to, py, pz),
            device_id_type=MESH,
        )

    def local(self, plane):
        tm, _, _, _ = place()
        part = self.rows(tm, plane)
        return pltpu.make_async_copy(
            self.source.at[part, :], self.target.at[part, :], self.own.at[plane]
        )


def whole_kernel(
    fields_hbm, fore_x_hbm, back_x_hbm, fore_y_hbm, back_y_hbm, fore_z_hbm, back_z_hbm,
    into4,
    fields, fore_x, back_x, fore_y, back_y, fore_z, back_z,
    load_sem, table_sem,
    out0, into0, send0, receive0, own0,
    out1, into1, send1, receive1, own1,
    out2, into2, send2, receive2, own2,
    out3, into3, send3, receive3, own3,
    out4, send4, receive4, own4,
    planes, first_modes, second_modes, start, fine, moved, matrix,
    coarse_out, coarse_in, coarse_send, coarse_receive, coarse_own,
    carry_out, carry_in, carry_send, carry_receive, carry_own,
):
    tm, py, pz, me = place()
    slices = lax.axis_size("tm")
    empty = jnp.zeros((2 * BLOCK, N), jnp.float32)
    into1[pl.ds(GRID_ROWS - 2 * BLOCK, 2 * BLOCK), :] = empty
    into4[pl.ds(GRID_ROWS - 2 * BLOCK, 2 * BLOCK), :] = empty
    coarse_in[...] = jnp.zeros_like(coarse_in)
    barrier = pltpu.get_barrier_semaphore()

    def greet(i, carry):
        peer = (tm, (py + i // 4) % 4, (pz + i % 4) % 4)
        pl.semaphore_signal(barrier, inc=1, device_id=peer, device_id_type=MESH)
        return carry

    lax.fori_loop(1, GROUP, greet, 0)

    def greet_slices(i, carry):
        peer = ((tm + i) % slices, py, pz)
        pl.semaphore_signal(barrier, inc=1, device_id=peer, device_id_type=MESH)
        return carry

    lax.fori_loop(1, slices, greet_slices, 0)

    loads = [
        pltpu.make_async_copy(held, ref, table_sem.at[i])
        for i, (held, ref) in enumerate(
            [
                (fore_x_hbm, fore_x),
                (fore_y_hbm, fore_y),
                (fore_z_hbm, fore_z),
                (back_z_hbm, back_z),
                (back_y_hbm, back_y),
                (back_x_hbm, back_x),
            ]
        )
    ]
    loads[0].start()

    def field_load(step):
        lines = pl.ds(pl.multiple_of(step * STEP, STEP), STEP)
        return pltpu.make_async_copy(
            fields_hbm.at[:, lines], fields.at[:, lines], load_sem.at[step]
        )

    def load(step, carry):
        field_load(step).start()
        return carry

    lax.fori_loop(0, BLOCK // STEP, load, 0)
    for copy in loads[1:]:
        copy.start()
    loads[0].wait()

    analysed = Exchange((out0, into0, send0, receive0, own0), True)
    to_grid = Exchange((out1, into1, send1, receive1, own1), False)
    to_modes = (
        Exchange((out2, into2, send2, receive2, own2), True),
        Exchange((out3, into3, send3, receive3, own3), True),
    )
    final = Exchange((out4, into4, send4, receive4, own4), False)
    coarse = Passing((coarse_out, coarse_in, coarse_send, coarse_receive, coarse_own))
    back = Passing((carry_out, carry_in, carry_send, carry_receive, carry_own))
    coarse_second = me + GROUP <= KCO

    def has_coarse(plane):
        return me + GROUP * plane <= KCO

    def analyse(step, carry):
        first = step * STEP
        field_load(step).wait()
        rows = [fields[f, first + y] for y in range(STEP) for f in range(4)]
        store_modes_x(jnp.concatenate(rows), fore_x, out0, first, STEP)
        return carry

    lax.fori_loop(0, BLOCK // STEP, analyse, 0)
    pl.semaphore_wait(barrier, GROUP - 1 + slices - 1)
    for plane in range(PLANES):
        analysed.start(plane)
    for copy in loads[1:]:
        copy.wait()

    def first_pass(plane, carry):
        analysed.arrived(plane)

        @pl.when(me + GROUP * plane <= KMAX)
        def _():
            first_modes[...] = fore_plane(into0, plane, planes, fore_y, fore_z)
            waves = waves_at(plane)
            inverse = 1.0 / jnp.maximum(squared(waves), 1.0)
            for part in range(2):
                lanes = slice(part * N, (part + 1) * N)
                state = [first_modes[f * KY : (f + 1) * KY, lanes] for f in range(4)]
                for f, value in enumerate(project(state[:3], waves, inverse) + (state[3],)):
                    start[plane, pl.ds(f * KY, KY), lanes] = value
            back_plane(start[plane], plane, out1, back_y, back_z)
            to_grid.start(plane)

        return carry

    lax.fori_loop(0, PLANES, first_pass, 0)

    def move(plane, carry):
        @pl.when(has_coarse(plane) & (tm > 0))
        def _():
            waves = coarse_waves(plane, FIRST_ROW, COARSE_ROWS)
            before = tuple(packed(start, plane, f) for f in range(4))
            for f, value in enumerate(propagate(before, waves)):
                moved[plane, f] = value

        @pl.when(has_coarse(plane) & (tm == 0))
        def _():
            moved[plane] = jnp.zeros((4, COARSE_ROWS, N), jnp.float32)

        waves = coarse_waves(plane, FIRST_ROW + tm * 8, 8)
        keep = coarse_inside(waves).astype(jnp.float32)
        zero = jnp.zeros((8, N), jnp.float32)
        for f in range(4):
            unit = tuple(zero + (1.0 if g == f else 0.0) for g in range(4))
            for g, value in enumerate(propagate(unit, waves)):
                matrix[plane, g * 4 + f] = keep * value
        return carry

    lax.fori_loop(0, 2, move, 0)

    def gather(plane, carry):
        to_grid.arrived(plane)
        return carry

    lax.fori_loop(0, PLANES, gather, 0)

    def lines(step, carry):
        first = step * STEP
        grid = load_fields_x(into1, back_x, first, STEP)
        one, two = [], []
        for y in range(STEP):
            u, v, w, b = (
                grid[y * N + f * BLOCK : y * N + (f + 1) * BLOCK] for f in range(4)
            )
            rest = w * w
            one += [u * u - rest, v * v - rest, u * v, u * w]
            two += [v * w, u * b, v * b, w * b]
        store_modes_x(jnp.concatenate(one), fore_x, out2, first, STEP)
        store_modes_x(jnp.concatenate(two), fore_x, out3, first, STEP)
        return carry

    lax.fori_loop(0, BLOCK // STEP, lines, 0)
    for plane in range(PLANES):
        for exchange in to_modes:
            exchange.start(plane)

    def second_pass(plane, carry):
        for exchange in to_modes:
            exchange.arrived(plane)

        @pl.when(me + GROUP * plane <= KMAX)
        def _():
            first_modes[...] = fore_plane(into2, plane, planes, fore_y, fore_z)
            second_modes[...] = fore_plane(into3, plane, planes, fore_y, fore_z)
            waves = waves_at(plane)
            wave_x, wave_y, wave_z = waves
            square = squared(waves)
            inverse = 1.0 / jnp.maximum(square, 1.0)
            for part in range(2):
                lanes = slice(part * N, (part + 1) * N)
                other = slice((1 - part) * N, (2 - part) * N)
                sign = 1.0 if part == 0 else -1.0
                xx, yy, xy, xz = (first_modes[f * KY : (f + 1) * KY, other] for f in range(4))
                yz, bx, by, bz = (second_modes[f * KY : (f + 1) * KY, other] for f in range(4))
                state = [start[plane, pl.ds(f * KY, KY), lanes] for f in range(4)]
                change = (
                    sign * (wave_x * xx + wave_y * xy + wave_z * xz),
                    sign * (wave_x * xy + wave_y * yy + wave_z * yz),
                    sign * (wave_x * xz + wave_y * yz),
                )
                lifted = sign * (wave_x * bx + wave_y * by + wave_z * bz)
                pushed = project(
                    (
                        change[0] + coriolis * state[1],
                        change[1] - coriolis * state[0],
                        change[2] + state[3],
                    ),
                    waves,
                    inverse,
                )
                rates = [pushed[f] - viscosity * square * state[f] for f in range(3)]
                rates.append(
                    lifted - buoyancy_square * state[2] - diffusivity * square * state[3]
                )
                for f in range(4):
                    fine[plane, pl.ds(f * KY, KY), lanes] = state[f] + time_step * rates[f]

        @pl.when(has_coarse(plane))
        def _():
            waves = coarse_waves(plane, FIRST_ROW, COARSE_ROWS)
            keep = coarse_inside(waves).astype(jnp.float32)
            for f in range(4):
                here = keep * packed(fine, plane, f) - keep * moved[plane, f]
                for tile in range(SCAN):
                    at = pl.multiple_of((plane * slices + tile) * TILE + f * 8, 8)
                    coarse_out[pl.ds(at, 8), :] = here[tile * 8 : tile * 8 + 8]

            def go(i, carry):
                @pl.when((tm + i) % slices < SCAN)
                def _():
                    coarse.remote(i, plane, False).start()

                return carry

            lax.fori_loop(1, slices, go, 0)

            @pl.when(tm < SCAN)
            def _():
                coarse.local(plane).start()

        @pl.when((plane == 1) & (tm < SCAN))
        def _():
            def wait(which):
                def go(i, carry):
                    coarse.remote(i, which, True).wait_recv()
                    return carry

                lax.fori_loop(1, slices, go, 0)
                coarse.local(which).wait()

            wait(0)

            @pl.when(coarse_second)
            def _():
                wait(1)

            def rows(n, which, f):
                return pl.ds(pl.multiple_of((which * slices + n) * TILE + f * 8, 8), 8)

            def step(n, state):
                new = []
                for which in range(2):
                    held = state[which * 4 : which * 4 + 4]
                    for g in range(4):
                        value = coarse_in[rows(n, which, g), :]
                        for f in range(4):
                            value = value + matrix[which, g * 4 + f] * held[f]
                        carry_out[rows(n, which, g), :] = value
                        new.append(value)
                return tuple(new)

            lax.fori_loop(0, slices, step, tuple([jnp.zeros((8, N), jnp.float32)] * 8))

            def send(which):
                def go(i, carry):
                    back.remote(i, which, False).start()
                    return carry

                lax.fori_loop(1, slices, go, 0)
                back.local(which).start()

            send(0)

            @pl.when(coarse_second)
            def _():
                send(1)

        return carry

    lax.fori_loop(0, PLANES, second_pass, 0)

    def last_pass(step, carry):
        plane = PLANES - 1 - step

        @pl.when(me + GROUP * plane <= KMAX)
        def _():
            @pl.when((plane < 2) & has_coarse(plane))
            def _():
                def wait(i, carry):
                    @pl.when((tm + slices - i) % slices < SCAN)
                    def _():
                        back.remote(i, plane, True).wait_recv()

                    return carry

                lax.fori_loop(1, slices, wait, 0)

                @pl.when(tm < SCAN)
                def _():
                    back.local(plane).wait()

                waves = coarse_waves(plane, FIRST_ROW, COARSE_ROWS)
                lane = lax.broadcasted_iota(jnp.int32, (COARSE_ROWS, N), 1)
                here = coarse_inside(waves) & (lane < 64)
                for f in range(4):
                    tiles = []
                    for tile in range(SCAN):
                        at = pl.multiple_of((plane * slices + tile) * TILE + f * 8, 8)
                        tiles.append(carry_in[pl.ds(at, 8), :])
                    value = jnp.concatenate(tiles)
                    rows = pl.ds(f * KY + FIRST_ROW, COARSE_ROWS)
                    fine[plane, rows, :N] = jnp.where(here, value, fine[plane, rows, :N])
                    fine[plane, rows, N:] = jnp.where(
                        here, pltpu.roll(value, 64, 1), fine[plane, rows, N:]
                    )

            back_plane(fine[plane], plane, out4, back_y, back_z)
            final.start(plane)

        return carry

    lax.fori_loop(0, PLANES, last_pass, 0)

    def done(plane, carry):
        analysed.sent(plane)
        to_grid.sent(plane)
        for exchange in to_modes:
            exchange.sent(plane)
        final.sent(plane)
        final.arrived(plane)
        return carry

    lax.fori_loop(0, PLANES, done, 0)

    def passed(q, carry):
        plane, i = q // slices, q % slices

        @pl.when((i > 0) & has_coarse(plane))
        def _():
            @pl.when((tm + i) % slices < SCAN)
            def _():
                coarse.remote(i, plane, False).wait_send()

            @pl.when(tm < SCAN)
            def _():
                back.remote(i, plane, False).wait_send()

        return carry

    lax.fori_loop(0, 2 * slices, passed, 0)


def lines_kernel(modes, back_x, out):
    grid = load_fields_x(modes, back_x, pl.program_id(0) * STEP, STEP)
    for y in range(STEP):
        for f in range(4):
            at = y * N + f * BLOCK
            out[f, y] = grid[at : at + BLOCK]


def on_device(state_old):
    slices = lax.axis_size("tm")
    fields = state_old[0]
    held = [jnp.asarray(table) for table in tables()]
    inputs = [pltpu.with_memory_space_constraint(a, pltpu.HBM) for a in [fields] + held]
    half = pltpu.VMEM((4 * KY, 2 * N), jnp.float32)
    modes = pltpu.VMEM((PLANES, 4 * KY, 2 * N), jnp.float32)
    passing = [
        pltpu.VMEM((2 * slices * TILE, N), jnp.float32),
        pltpu.VMEM((2 * slices * TILE, N), jnp.float32),
        pltpu.SemaphoreType.DMA((2 * slices,)),
        pltpu.SemaphoreType.DMA((2 * slices,)),
        pltpu.SemaphoreType.DMA((2,)),
    ]
    last = exchange_scratch(False)
    arrived = pl.pallas_call(
        whole_kernel,
        name="whole",
        out_shape=jax.ShapeDtypeStruct((GRID_ROWS, N), jnp.float32),
        in_specs=[pl.BlockSpec(memory_space=pltpu.HBM)] * len(inputs),
        out_specs=pl.BlockSpec(memory_space=pltpu.VMEM),
        scratch_shapes=[pltpu.VMEM(a.shape, a.dtype) for a in inputs]
        + [
            pltpu.SemaphoreType.DMA((BLOCK // STEP,)),
            pltpu.SemaphoreType.DMA((len(held),)),
        ]
        + exchange_scratch(True)
        + exchange_scratch(False)
        + exchange_scratch(True)
        + exchange_scratch(True)
        + [last[0]]
        + last[2:]
        + [
            pltpu.VMEM((2, 2 * N, 2 * N), jnp.float32),
            half,
            half,
            modes,
            modes,
            pltpu.VMEM((2, 4, COARSE_ROWS, N), jnp.float32),
            pltpu.VMEM((2, 16, 8, N), jnp.float32),
        ]
        + passing
        + passing,
        compiler_params=pltpu.CompilerParams(
            collective_id=0, has_side_effects=True, vmem_limit_bytes=VMEM_BYTES
        ),
    )(*inputs)
    result = pl.pallas_call(
        lines_kernel,
        name="lines",
        grid=(BLOCK // STEP,),
        out_shape=jax.ShapeDtypeStruct(fields.shape, jnp.float32),
        in_specs=[pl.BlockSpec(memory_space=pltpu.VMEM)] * 2,
        out_specs=pl.BlockSpec((4, STEP, BLOCK, N), lambda i: (0, i, 0, 0)),
        compiler_params=pltpu.CompilerParams(vmem_limit_bytes=16 << 20),
    )(arrived, held[1])
    return result[None]


def solution(mesh):
    return jax.shard_map(
        on_device,
        mesh=mesh,
        in_specs=(P("tm", None, "py", "pz", None),),
        out_specs=P("tm", None, "py", "pz", None),
        check_vma=False,
    )
```

time: 148 us -> 118 us (0.80)
  Pallas kernels: 140 us -> 116 us
  local copies, waits for them, and re-layouts: 7.47 us -> 0.01 us
    pallas_call x3 -> x2, Pallas kernels: 140 us -> 116 us  [the longest x1 112 us: on_device(): pl.pallas_call(whole_kernel, name='whole', out_shape=jax.ShapeDtypeStruct...]
    unnamed x17 -> x2, local copies, waits for them, and re-layouts: 7.47 us -> 0.01 us
where the time goes in v2:
time: 118 us; the launch traced here: 116 us
  Pallas kernels  116 us (98%)
    pallas_call x1, Pallas kernels, on_device(): pl.pallas_call(whole_kernel, name='whole', out_shape=jax.ShapeDtypeStruct...  112 us
    pallas_call x1, Pallas kernels, on_device(): pl.pallas_call(lines_kernel, name='lines', grid=(BLOCK // STEP,), out_sha...  4.48 us

profile of v2, /device:TPU:1, one launch (start us, length us, event | category | flops | bytes accessed | tf_op | source)
XLA Modules:
  0.0 116.5 jit_solution(5891283197147918898)
XLA Ops:
  0.0 0.0 copy-start
  0.0 112.0 %whole.1.modes = f32[2816,128]{1,0:T(8,128)S(1)} custom-call(f32[4,32,32,128]{3,2,1,0:T(8,128)} %bitcast.2, bf16[256,256]{1,0:T(8,128)(2,1)} %constant.12.clone.fore_x_hbm, bf16[256,256]{1,0:T(8,128)(2,1)} %constant.13.clone.back_x_hbm.back_x, bf16[384,256]{1,0:T(8,128)(2,1)} %constant.14.clone.fore_y_hbm, bf16[512,192]{1,0:T(8,128)(2,1)} %constant.15.clone.back_y_hbm, ...), custom_call_target="tpu_custom_call" | custom-call | tf_op jit(solution)/shard_map/whole/pallas_call | solution.py:771
  112.0 0.0 copy-done
  112.0 4.5 %lines.1 = f32[4,32,32,128]{3,2,1,0:T(8,128)} custom-call(f32[2816,128]{1,0:T(8,128)S(1)} %whole.1.modes, bf16[256,256]{1,0:T(8,128)(2,1)S(1)} %copy-done), custom_call_target="tpu_custom_call" | custom-call | tf_op jit(solution)/shard_map/lines/pallas_call | solution.py:803
Async XLA Ops:
  0.0 112.0 %copy-start = (bf16[256,256]{1,0:T(8,128)(2,1)S(1)}, bf16[256,256]{1,0:T(8,128)(2,1)}, u32[]{:S(2)}) copy-start(bf16[256,256]{1,0:T(8,128)(2,1)} %constant.13.clone.back_x_hbm.back_x) | copy-start | bytes 393220

commit v3 on v2

--- a/solution.py
+++ b/solution.py
@@ -17,9 +17,19 @@
 BLOCK = 32
 MODE_ROWS = 88
 HOLDERS = KMAX + 1 - 2 * GROUP
+KZ = 2 * KMAX + 1
+EMPTY = PLANES * GROUP - KMAX - 1
+THIN = N // GROUP
+SYNTH_PACKS = 6
+PRODUCT_PACKS = 11
+SPECTRAL_ROWS = 2 * PLANES * GROUP * BLOCK
 GRID_ROWS = MODE_ROWS * BLOCK
 PLANE_ROWS = PLANES * GROUP * 2 * BLOCK
 SCAN = 6
+ORDER = (
+    (2, 2), (2, 3), (1, 2), (3, 2), (1, 3), (3, 3), (2, 0), (2, 1),
+    (0, 2), (0, 3), (1, 0), (3, 0), (1, 1), (3, 1), (0, 1),
+)
 MESH = pl.DeviceIdType.MESH
 VMEM_BYTES = 50 << 20
 
@@ -132,29 +142,31 @@
     return tm, py, pz, py * 4 + pz
 
 
-def chunk(owner, plane):
-    rows = 2 * BLOCK
-    return pl.ds(pl.multiple_of((plane * GROUP + owner) * rows, rows), rows)
+def rows_at(start, count):
+    return pl.ds(pl.multiple_of(start, 8), count)
 
 
 class Exchange:
-    def __init__(self, refs, to_modes):
+    def __init__(self, refs, to_modes, rows):
         self.source, self.target, self.send, self.receive, self.own = refs
-        self.to_modes = to_modes
+        self.to_modes, self.rows = to_modes, rows
+
+    def chunk(self, owner, plane):
+        return rows_at((plane * GROUP + owner) * self.rows, self.rows)
 
     def local(self, plane):
         _, _, _, me = place()
-        part = chunk(me, plane)
+        part = self.chunk(me, plane)
         return pltpu.make_async_copy(
             self.source.at[part, :], self.target.at[part, :], self.own.at[plane]
         )
 
-    def remote(self, i, plane):
+    def remote(self, step, plane):
         tm, py, pz, me = place()
-        to_y, to_z = (py + i // 4) % 4, (pz + i % 4) % 4
+        to_y, to_z = (py + step[0]) % 4, (pz + step[1]) % 4
         return pltpu.make_async_remote_copy(
-            src_ref=self.source.at[chunk(to_y * 4 + to_z, plane), :],
-            dst_ref=self.target.at[chunk(me, plane), :],
+            src_ref=self.source.at[self.chunk(to_y * 4 + to_z, plane), :],
+            dst_ref=self.target.at[self.chunk(me, plane), :],
             send_sem=self.send.at[plane],
             recv_sem=self.receive.at[plane],
             device_id=(tm, to_y, to_z),
@@ -163,7 +175,7 @@
 
     def amount(self, count, plane):
         tm, py, pz, _ = place()
-        rows = pl.ds(0, count * 2 * BLOCK)
+        rows = pl.ds(0, count * self.rows)
         return pltpu.make_async_remote_copy(
             src_ref=self.source.at[rows, :],
             dst_ref=self.target.at[rows, :],
@@ -176,20 +188,24 @@
     def start(self, plane):
         _, py, pz, me = place()
 
-        def go(i, carry):
-            to = (py + i // 4) % 4 * 4 + (pz + i % 4) % 4
-            wanted = (to if self.to_modes else me) + GROUP * plane <= KMAX
-
-            @pl.when(wanted)
-            def _():
-                self.remote(i, plane).start()
-
-            return carry
-
-        lax.fori_loop(1, GROUP, go, 0)
+        def go(step):
+            to = (py + step[0]) % 4 * 4 + (pz + step[1]) % 4
+            if not self.to_modes or (isinstance(plane, int) and plane < PLANES - 1):
+                self.remote(step, plane).start()
+            else:
+                pl.when(to + GROUP * plane <= KMAX)(lambda: self.remote(step, plane).start())
+
+        def all_steps():
+            for step in ORDER:
+                go(step)
+
+        if self.to_modes:
+            all_steps()
 
         @pl.when(me + GROUP * plane <= KMAX)
         def _():
+            if not self.to_modes:
+                all_steps()
             self.local(plane).start()
 
     def modes_side(self, plane, done):
@@ -228,9 +244,7 @@
         side(plane, lambda copy: copy.wait_send())
 
 
-def exchange_scratch(to_modes):
-    sizes = (GRID_ROWS, PLANE_ROWS)
-    source, target = sizes if to_modes else sizes[::-1]
+def exchange_scratch(source, target):
     return [
         pltpu.VMEM((source, N), jnp.float32),
         pltpu.VMEM((target, N), jnp.float32),
@@ -240,17 +254,17 @@
     ]
 
 
-def store_modes_x(fields, table, target, first, count):
+def store_modes_x(fields, table, target, first, count, gap=1):
     modes = by_x(fields, table)
     for y in range(count):
         turned = modes[y * N : (y + 1) * N].T
-        target[pl.ds(first + y, MODE_ROWS, stride=BLOCK), :] = turned[:MODE_ROWS]
-
-
-def load_fields_x(source, table, first, count):
+        target[pl.ds(first + y * gap, MODE_ROWS, stride=BLOCK), :] = turned[:MODE_ROWS]
+
+
+def load_fields_x(source, table, first, count, gap=1):
     lines = []
     for y in range(count):
-        rows = source[pl.ds(first + y, MODE_ROWS, stride=BLOCK), :]
+        rows = source[pl.ds(first + y * gap, MODE_ROWS, stride=BLOCK), :]
         rows = jnp.concatenate([rows, jnp.zeros((N - MODE_ROWS, N), jnp.float32)])
         lines.append(rows.T)
     return by_x(jnp.concatenate(lines), table)
@@ -293,6 +307,113 @@
                 target[pl.ds(pl.multiple_of(start, BLOCK), BLOCK), :] = piece
 
 
+def pack(pieces):
+    out = []
+    whole = len(pieces) // 3 * 3
+    for first in range(0, whole, 3):
+        one, two, three = pieces[first : first + 3]
+        lane = lax.broadcasted_iota(jnp.int32, one.shape, 1)
+        turned = pltpu.roll(two, KZ, 1)
+        out.append(jnp.where(lane < KZ, one, turned))
+        out.append(jnp.where(lane < 2 * KZ - N, turned, pltpu.roll(three, 2 * KZ - N, 1)))
+    return out + list(pieces[whole:])
+
+
+def unpack(packs, count):
+    out = []
+    for first in range(0, count // 3 * 2, 2):
+        one, two = packs[first : first + 2]
+        lane = lax.broadcasted_iota(jnp.int32, one.shape, 1)
+        out.append(one)
+        out.append(pltpu.roll(jnp.where(lane < 2 * KZ - N, two, one), N - KZ, 1))
+        out.append(pltpu.roll(two, 2 * N - 2 * KZ, 1))
+    return out + list(packs[count // 3 * 2 :])
+
+
+def beside(left, right):
+    return jnp.concatenate([left, right], axis=1)
+
+
+def spread_packs(packs, plane, target):
+    for owner in range(GROUP):
+        for k, values in enumerate(packs):
+            start = ((plane * GROUP + owner) * len(packs) + k) * THIN
+            target[rows_at(start, THIN), :] = values[owner * THIN : (owner + 1) * THIN]
+
+
+def gather_packs(source, plane, count):
+    packs = []
+    for k in range(count):
+        starts = [((plane * GROUP + owner) * count + k) * THIN for owner in range(GROUP)]
+        packs.append(jnp.concatenate([source[rows_at(at, THIN), :] for at in starts]))
+    return packs
+
+
+def back_along_y(values, plane, target, back_y):
+    pieces = []
+    for duo in range(2):
+        both = []
+        for f in (2 * duo, 2 * duo + 1):
+            own = values[f * KY : (f + 1) * KY]
+            both.append(jnp.concatenate([own[:, :N], own[:, N:]]))
+        along = by_left(back_y, beside(*both))
+        pieces += [along[:N, :N], along[N:, :N], along[:N, N:], along[N:, N:]]
+    spread_packs(pack(pieces), plane, target)
+
+
+def back_along_z(source, plane, spectral, back_z):
+    pieces = unpack(gather_packs(source, plane, SYNTH_PACKS), 8)
+    lines = [beside(pieces[2 * f], pieces[2 * f + 1]) for f in range(4)]
+    along = by_right(jnp.concatenate(lines), back_z)
+    for owner in range(GROUP):
+        for f in range(4):
+            rows = slice(f * N + owner * THIN, f * N + (owner + 1) * THIN)
+            for c in range(2):
+                start = ((plane * GROUP + owner) * 2 + c) * BLOCK + f * THIN
+                spectral[rows_at(start, THIN), :] = along[rows, c * N : (c + 1) * N]
+
+
+def fore_along_z(spectral, plane, target, fore_z):
+    pieces = []
+    for ref in spectral:
+        lines = []
+        for owner in range(GROUP):
+            start = (plane * GROUP + owner) * 2 * BLOCK
+            both = [ref[rows_at(start + c * BLOCK, BLOCK), :] for c in range(2)]
+            lines.append(beside(*both))
+        along = by_right(jnp.concatenate(lines), fore_z)
+        for f in range(4):
+            for c in range(2):
+                pieces.append(
+                    jnp.concatenate(
+                        [
+                            along[
+                                owner * BLOCK + f * THIN : owner * BLOCK + (f + 1) * THIN,
+                                c * N : (c + 1) * N,
+                            ]
+                            for owner in range(GROUP)
+                        ]
+                    )
+                )
+    spread_packs(pack(pieces), plane, target)
+
+
+def fore_along_y(source, plane, modes, fore_y):
+    pieces = unpack(gather_packs(source, plane, PRODUCT_PACKS), 16)
+    for duo in range(4):
+        both = [
+            jnp.concatenate([pieces[2 * f], pieces[2 * f + 1]])
+            for f in (2 * duo, 2 * duo + 1)
+        ]
+        along = by_left(fore_y, beside(*both))
+        ref = modes[duo // 2]
+        for half in range(2):
+            rows = slice((duo % 2 * 2 + half) * KY, (duo % 2 * 2 + half + 1) * KY)
+            own = along[:, half * N : (half + 1) * N]
+            ref[rows, :N] = own[:KY]
+            ref[rows, N:] = own[KY:]
+
+
 def waves_at(plane):
     _, _, _, me = place()
     wave_x = (me + GROUP * plane).astype(jnp.float32)
@@ -404,8 +525,8 @@
     out0, into0, send0, receive0, own0,
     out1, into1, send1, receive1, own1,
     out2, into2, send2, receive2, own2,
-    out3, into3, send3, receive3, own3,
     out4, send4, receive4, own4,
+    synth, first_products, second_products,
     planes, first_modes, second_modes, start, fine, moved, matrix,
     coarse_out, coarse_in, coarse_send, coarse_receive, coarse_own,
     carry_out, carry_in, carry_send, carry_receive, carry_own,
@@ -413,7 +534,9 @@
     tm, py, pz, me = place()
     slices = lax.axis_size("tm")
     empty = jnp.zeros((2 * BLOCK, N), jnp.float32)
-    into1[pl.ds(GRID_ROWS - 2 * BLOCK, 2 * BLOCK), :] = empty
+    into1[pl.ds((KMAX + 1) * SYNTH_PACKS * THIN, EMPTY * SYNTH_PACKS * THIN), :] = jnp.zeros(
+        (EMPTY * SYNTH_PACKS * THIN, N), jnp.float32
+    )
     into4[pl.ds(GRID_ROWS - 2 * BLOCK, 2 * BLOCK), :] = empty
     coarse_in[...] = jnp.zeros_like(coarse_in)
     barrier = pltpu.get_barrier_semaphore()
@@ -462,13 +585,10 @@
         copy.start()
     loads[0].wait()
 
-    analysed = Exchange((out0, into0, send0, receive0, own0), True)
-    to_grid = Exchange((out1, into1, send1, receive1, own1), False)
-    to_modes = (
-        Exchange((out2, into2, send2, receive2, own2), True),
-        Exchange((out3, into3, send3, receive3, own3), True),
-    )
-    final = Exchange((out4, into4, send4, receive4, own4), False)
+    analysed = Exchange((out0, into0, send0, receive0, own0), True, 2 * BLOCK)
+    to_grid = Exchange((out1, into1, send1, receive1, own1), False, SYNTH_PACKS * THIN)
+    to_modes = Exchange((out2, into2, send2, receive2, own2), True, PRODUCT_PACKS * THIN)
+    final = Exchange((out4, into4, send4, receive4, own4), False, 2 * BLOCK)
     coarse = Passing((coarse_out, coarse_in, coarse_send, coarse_receive, coarse_own))
     back = Passing((carry_out, carry_in, carry_send, carry_receive, carry_own))
     coarse_second = me + GROUP <= KCO
@@ -503,7 +623,7 @@
                 state = [first_modes[f * KY : (f + 1) * KY, lanes] for f in range(4)]
                 for f, value in enumerate(project(state[:3], waves, inverse) + (state[3],)):
                     start[plane, pl.ds(f * KY, KY), lanes] = value
-            back_plane(start[plane], plane, out1, back_y, back_z)
+            back_along_y(start[plane], plane, out1, back_y)
             to_grid.start(plane)
 
         return carry
@@ -535,38 +655,36 @@
 
     def gather(plane, carry):
         to_grid.arrived(plane)
+        back_along_z(into1, plane, synth, back_z)
         return carry
 
     lax.fori_loop(0, PLANES, gather, 0)
 
-    def lines(step, carry):
-        first = step * STEP
-        grid = load_fields_x(into1, back_x, first, STEP)
-        one, two = [], []
-        for y in range(STEP):
-            u, v, w, b = (
-                grid[y * N + f * BLOCK : y * N + (f + 1) * BLOCK] for f in range(4)
-            )
-            rest = w * w
-            one += [u * u - rest, v * v - rest, u * v, u * w]
-            two += [v * w, u * b, v * b, w * b]
-        store_modes_x(jnp.concatenate(one), fore_x, out2, first, STEP)
-        store_modes_x(jnp.concatenate(two), fore_x, out3, first, STEP)
-        return carry
-
-    lax.fori_loop(0, BLOCK // STEP, lines, 0)
-    for plane in range(PLANES):
-        for exchange in to_modes:
-            exchange.start(plane)
+    def lines(y, carry):
+        grid = load_fields_x(synth, back_x, y, 4, THIN)
+        u, v, w, b = (grid[f * N : (f + 1) * N] for f in range(4))
+        rest = w * w
+        one = [u * u - rest, v * v - rest, u * v, u * w]
+        two = [v * w, u * b, v * b, w * b]
+        store_modes_x(jnp.concatenate(one), fore_x, first_products, y, 4, THIN)
+        store_modes_x(jnp.concatenate(two), fore_x, second_products, y, 4, THIN)
+        return carry
+
+    lax.fori_loop(0, THIN, lines, 0)
+
+    def scatter(plane, carry):
+        fore_along_z((first_products, second_products), plane, out2, fore_z)
+        to_modes.start(plane)
+        return carry
+
+    lax.fori_loop(0, PLANES, scatter, 0)
 
     def second_pass(plane, carry):
-        for exchange in to_modes:
-            exchange.arrived(plane)
+        to_modes.arrived(plane)
 
         @pl.when(me + GROUP * plane <= KMAX)
         def _():
-            first_modes[...] = fore_plane(into2, plane, planes, fore_y, fore_z)
-            second_modes[...] = fore_plane(into3, plane, planes, fore_y, fore_z)
+            fore_along_y(into2, plane, (first_modes, second_modes), fore_y)
             waves = waves_at(plane)
             wave_x, wave_y, wave_z = waves
             square = squared(waves)
@@ -719,8 +837,7 @@
     def done(plane, carry):
         analysed.sent(plane)
         to_grid.sent(plane)
-        for exchange in to_modes:
-            exchange.sent(plane)
+        to_modes.sent(plane)
         final.sent(plane)
         final.arrived(plane)
         return carry
@@ -767,7 +884,10 @@
         pltpu.SemaphoreType.DMA((2 * slices,)),
         pltpu.SemaphoreType.DMA((2,)),
     ]
-    last = exchange_scratch(False)
+    last = exchange_scratch(PLANE_ROWS, GRID_ROWS)
+    synth_rows = PLANES * GROUP * SYNTH_PACKS * THIN
+    product_rows = PLANES * GROUP * PRODUCT_PACKS * THIN
+    spectral = pltpu.VMEM((SPECTRAL_ROWS, N), jnp.float32)
     arrived = pl.pallas_call(
         whole_kernel,
         name="whole",
@@ -779,12 +899,12 @@
             pltpu.SemaphoreType.DMA((BLOCK // STEP,)),
             pltpu.SemaphoreType.DMA((len(held),)),
         ]
-        + exchange_scratch(True)
-        + exchange_scratch(False)
-        + exchange_scratch(True)
-        + exchange_scratch(True)
+        + exchange_scratch(GRID_ROWS, PLANE_ROWS)
+        + exchange_scratch(synth_rows, synth_rows)
+        + exchange_scratch(product_rows, product_rows)
         + [last[0]]
         + last[2:]
+        + [spectral, spectral, spectral]
         + [
             pltpu.VMEM((2, 2 * N, 2 * N), jnp.float32),
             half,

time: 118 us -> 103 us (0.87)
  Pallas kernels: 116 us -> 102 us
    pallas_call x1, Pallas kernels: 112 us -> 98 us  [on_device(): pl.pallas_call(whole_kernel, name='whole', out_shape=jax.ShapeDtypeStruct...]
where the time goes in v3:
time: 103 us; the launch traced here: 102 us
  Pallas kernels  102 us (99%)
    pallas_call x1, Pallas kernels, on_device(): pl.pallas_call(whole_kernel, name='whole', out_shape=jax.ShapeDtypeStruct...  98 us
    pallas_call x1, Pallas kernels, on_device(): pl.pallas_call(lines_kernel, name='lines', grid=(BLOCK // STEP,), out_sha...  4.48 us

profile of v3, /device:TPU:1, one launch (start us, length us, event | category | flops | bytes accessed | tf_op | source)
XLA Modules:
  0.0 102.5 jit_solution(15400098902807364521)
XLA Ops:
  0.0 0.0 copy-start
  0.0 98.0 %whole.1.modes = f32[2816,128]{1,0:T(8,128)S(1)} custom-call(f32[4,32,32,128]{3,2,1,0:T(8,128)} %bitcast.2, bf16[256,256]{1,0:T(8,128)(2,1)} %constant.12.clone.fore_x_hbm, bf16[256,256]{1,0:T(8,128)(2,1)} %constant.13.clone.back_x_hbm.back_x, bf16[384,256]{1,0:T(8,128)(2,1)} %constant.14.clone.fore_y_hbm, bf16[512,192]{1,0:T(8,128)(2,1)} %constant.15.clone.back_y_hbm, ...), custom_call_target="tpu_custom_call" | custom-call | tf_op jit(solution)/shard_map/whole/pallas_call | solution.py:891
  98.0 0.0 copy-done
  98.0 4.5 %lines.1 = f32[4,32,32,128]{3,2,1,0:T(8,128)} custom-call(f32[2816,128]{1,0:T(8,128)S(1)} %whole.1.modes, bf16[256,256]{1,0:T(8,128)(2,1)S(1)} %copy-done), custom_call_target="tpu_custom_call" | custom-call | tf_op jit(solution)/shard_map/lines/pallas_call | solution.py:923
Async XLA Ops:
  0.0 98.0 %copy-start = (bf16[256,256]{1,0:T(8,128)(2,1)S(1)}, bf16[256,256]{1,0:T(8,128)(2,1)}, u32[]{:S(2)}) copy-start(bf16[256,256]{1,0:T(8,128)(2,1)} %constant.13.clone.back_x_hbm.back_x) | copy-start | bytes 393220

commit v4 on v3

--- a/solution.py
+++ b/solution.py
@@ -11,7 +11,7 @@
 KMAX = 42
 KCO = 21
 N = 128
-KY = 96
+KY = 88
 PLANES = 3
 GROUP = 16
 BLOCK = 32
@@ -22,7 +22,8 @@
 THIN = N // GROUP
 SYNTH_PACKS = 6
 PRODUCT_PACKS = 11
-SPECTRAL_ROWS = 2 * PLANES * GROUP * BLOCK
+PITCH = BLOCK + 1
+SPECTRAL_ROWS = 2 * PLANES * GROUP * PITCH
 GRID_ROWS = MODE_ROWS * BLOCK
 PLANE_ROWS = PLANES * GROUP * 2 * BLOCK
 SCAN = 6
@@ -69,6 +70,15 @@
             ]
         )
 
+    def one_left(table):
+        high, low = halves(table)
+        return np.concatenate(
+            [
+                np.concatenate([high, high], axis=1),
+                np.concatenate([low, np.zeros_like(low)], axis=1),
+            ]
+        )
+
     def pair(slots):
         waves = np.arange(slots) - KMAX
         angle = 2 * np.pi / N * ((waves[:, None] * cells[None, :]) % N)
@@ -82,13 +92,15 @@
     fore_z = np.block([[cos_z.T, -sin_z.T], [sin_z.T, cos_z.T]])
     back_z = np.block([[cos_z, sin_z], [-sin_z, cos_z]])
     stack = lambda table: np.concatenate(halves(table))
+    slots = 2 * PLANES * GROUP
     return (
-        one_pass(fore),
-        one_pass(back),
+        one_left(fore.T[:slots]),
+        one_left(back[:slots].T),
         stack(fore_y),
         stack(back_y),
         stack(fore_z),
         stack(back_z),
+        one_pass(back),
     )
 
 
@@ -105,6 +117,20 @@
 def by_x(values, table):
     out = mul(jnp.concatenate(split(values), axis=1), table[...])
     return out[:, :N] + out[:, N:]
+
+
+def by_left_once(table, values):
+    rows = table.shape[0] // 2
+    out = mul(table[...], jnp.concatenate(split(values)))
+    return out[:rows] + out[rows:]
+
+
+def by_turned(table, values):
+    rows = table.shape[0] // 2
+    turned = (((1,), (1,)), ((), ()))
+    pair = jnp.concatenate(split(values), axis=1)
+    out = lax.dot_general(table[...], pair, turned, preferred_element_type=jnp.float32)
+    return out[:rows] + out[rows:]
 
 
 def by_left(table, values):
@@ -254,17 +280,10 @@
     ]
 
 
-def store_modes_x(fields, table, target, first, count, gap=1):
-    modes = by_x(fields, table)
-    for y in range(count):
-        turned = modes[y * N : (y + 1) * N].T
-        target[pl.ds(first + y * gap, MODE_ROWS, stride=BLOCK), :] = turned[:MODE_ROWS]
-
-
-def load_fields_x(source, table, first, count, gap=1):
+def load_fields_x(source, table, first, count):
     lines = []
     for y in range(count):
-        rows = source[pl.ds(first + y * gap, MODE_ROWS, stride=BLOCK), :]
+        rows = source[pl.ds(first + y, MODE_ROWS, stride=PITCH), :]
         rows = jnp.concatenate([rows, jnp.zeros((N - MODE_ROWS, N), jnp.float32)])
         lines.append(rows.T)
     return by_x(jnp.concatenate(lines), table)
@@ -369,8 +388,8 @@
         for f in range(4):
             rows = slice(f * N + owner * THIN, f * N + (owner + 1) * THIN)
             for c in range(2):
-                start = ((plane * GROUP + owner) * 2 + c) * BLOCK + f * THIN
-                spectral[rows_at(start, THIN), :] = along[rows, c * N : (c + 1) * N]
+                start = ((plane * GROUP + owner) * 2 + c) * PITCH + f * THIN
+                spectral[pl.ds(start, THIN), :] = along[rows, c * N : (c + 1) * N]
 
 
 def fore_along_z(spectral, plane, target, fore_z):
@@ -378,8 +397,8 @@
     for ref in spectral:
         lines = []
         for owner in range(GROUP):
-            start = (plane * GROUP + owner) * 2 * BLOCK
-            both = [ref[rows_at(start + c * BLOCK, BLOCK), :] for c in range(2)]
+            start = (plane * GROUP + owner) * 2 * PITCH
+            both = [ref[pl.ds(start + c * PITCH, BLOCK), :] for c in range(2)]
             lines.append(beside(*both))
         along = by_right(jnp.concatenate(lines), fore_z)
         for f in range(4):
@@ -462,6 +481,7 @@
 COARSE_ROWS = 8 * SCAN
 TILE = 8 * 4
 STEP = 4
+LINES = 16
 
 
 def coarse_waves(plane, row0, rows):
@@ -599,11 +619,17 @@
     def analyse(step, carry):
         first = step * STEP
         field_load(step).wait()
-        rows = [fields[f, first + y] for y in range(STEP) for f in range(4)]
-        store_modes_x(jnp.concatenate(rows), fore_x, out0, first, STEP)
+        for duo in range(STEP // 2):
+            rows = [fields[f, first + 2 * duo + y] for y in range(2) for f in range(4)]
+            modes = by_turned(fore_x, jnp.concatenate(rows))
+            for y in range(2):
+                own = modes[:MODE_ROWS, y * N : (y + 1) * N]
+                synth[pl.ds(first + 2 * duo + y, MODE_ROWS, stride=PITCH), :] = own
         return carry
 
     lax.fori_loop(0, BLOCK // STEP, analyse, 0)
+    for slot in range(MODE_ROWS):
+        out0[pl.ds(slot * BLOCK, BLOCK), :] = synth[pl.ds(slot * PITCH, BLOCK), :]
     pl.semaphore_wait(barrier, GROUP - 1 + slices - 1)
     for plane in range(PLANES):
         analysed.start(plane)
@@ -661,13 +687,25 @@
     lax.fori_loop(0, PLANES, gather, 0)
 
     def lines(y, carry):
-        grid = load_fields_x(synth, back_x, y, 4, THIN)
-        u, v, w, b = (grid[f * N : (f + 1) * N] for f in range(4))
+        slots = 2 * PLANES * GROUP
+
+        def modes_at(ref, f):
+            return ref.at[pl.ds(y + f * THIN, slots, stride=PITCH), :]
+
+        grid = []
+        for f in (0, 2):
+            both = beside(modes_at(synth, f)[...], modes_at(synth, f + 1)[...])
+            both = by_left_once(back_x, both)
+            grid += [both[:, :N], both[:, N:]]
+        u, v, w, b = grid
         rest = w * w
         one = [u * u - rest, v * v - rest, u * v, u * w]
         two = [v * w, u * b, v * b, w * b]
-        store_modes_x(jnp.concatenate(one), fore_x, first_products, y, 4, THIN)
-        store_modes_x(jnp.concatenate(two), fore_x, second_products, y, 4, THIN)
+        for ref, values in ((first_products, one), (second_products, two)):
+            for f in (0, 2):
+                both = by_left_once(fore_x, beside(values[f], values[f + 1]))
+                modes_at(ref, f)[...] = both[:, :N]
+                modes_at(ref, f + 1)[...] = both[:, N:]
         return carry
 
     lax.fori_loop(0, THIN, lines, 0)
@@ -862,9 +900,14 @@
     lax.fori_loop(0, 2 * slices, passed, 0)
 
 
-def lines_kernel(modes, back_x, out):
-    grid = load_fields_x(modes, back_x, pl.program_id(0) * STEP, STEP)
-    for y in range(STEP):
+def lines_kernel(modes, back_x, out, held):
+    @pl.when(pl.program_id(0) == 0)
+    def _():
+        for slot in range(MODE_ROWS):
+            held[pl.ds(slot * PITCH, BLOCK), :] = modes[pl.ds(slot * BLOCK, BLOCK), :]
+
+    grid = load_fields_x(held, back_x, pl.program_id(0) * LINES, LINES)
+    for y in range(LINES):
         for f in range(4):
             at = y * N + f * BLOCK
             out[f, y] = grid[at : at + BLOCK]
@@ -874,7 +917,8 @@
     slices = lax.axis_size("tm")
     fields = state_old[0]
     held = [jnp.asarray(table) for table in tables()]
-    inputs = [pltpu.with_memory_space_constraint(a, pltpu.HBM) for a in [fields] + held]
+    inner = held[:-1]
+    inputs = [pltpu.with_memory_space_constraint(a, pltpu.HBM) for a in [fields] + inner]
     half = pltpu.VMEM((4 * KY, 2 * N), jnp.float32)
     modes = pltpu.VMEM((PLANES, 4 * KY, 2 * N), jnp.float32)
     passing = [
@@ -897,7 +941,7 @@
         scratch_shapes=[pltpu.VMEM(a.shape, a.dtype) for a in inputs]
         + [
             pltpu.SemaphoreType.DMA((BLOCK // STEP,)),
-            pltpu.SemaphoreType.DMA((len(held),)),
+            pltpu.SemaphoreType.DMA((len(inner),)),
         ]
         + exchange_scratch(GRID_ROWS, PLANE_ROWS)
         + exchange_scratch(synth_rows, synth_rows)
@@ -923,12 +967,13 @@
     result = pl.pallas_call(
         lines_kernel,
         name="lines",
-        grid=(BLOCK // STEP,),
+        grid=(BLOCK // LINES,),
         out_shape=jax.ShapeDtypeStruct(fields.shape, jnp.float32),
         in_specs=[pl.BlockSpec(memory_space=pltpu.VMEM)] * 2,
-        out_specs=pl.BlockSpec((4, STEP, BLOCK, N), lambda i: (0, i, 0, 0)),
+        scratch_shapes=[pltpu.VMEM((MODE_ROWS * PITCH, N), jnp.float32)],
+        out_specs=pl.BlockSpec((4, LINES, BLOCK, N), lambda i: (0, i, 0, 0)),
         compiler_params=pltpu.CompilerParams(vmem_limit_bytes=16 << 20),
-    )(arrived, held[1])
+    )(arrived, held[-1])
     return result[None]
 
 

time: 103 us -> 96.8 us (0.940)
  Pallas kernels: 102 us -> 96.6 us
    pallas_call x1, Pallas kernels: 98 us -> 94.5 us  [on_device(): pl.pallas_call(whole_kernel, name='whole', out_shape=jax.ShapeDtypeStruct...]
    pallas_call x1, Pallas kernels: 4.48 us -> 2.13 us  [on_device(): pl.pallas_call(lines_kernel, name='lines', grid=(BLOCK // LINES,), out_sh...]
where the time goes in v4:
time: 96.8 us; the launch traced here: 96.7 us
  Pallas kernels  96.6 us (100%)
    pallas_call x1, Pallas kernels, on_device(): pl.pallas_call(whole_kernel, name='whole', out_shape=jax.ShapeDtypeStruct...  94.5 us
    pallas_call x1, Pallas kernels, on_device(): pl.pallas_call(lines_kernel, name='lines', grid=(BLOCK // LINES,), out_sh...  2.13 us

profile of v4, /device:TPU:1, one launch (start us, length us, event | category | flops | bytes accessed | tf_op | source)
XLA Modules:
  0.0 96.7 jit_solution(8164472024221979479)
XLA Ops:
  0.0 0.0 copy-start
  0.0 94.5 %whole.1.modes = f32[2816,128]{1,0:T(8,128)S(1)} custom-call(f32[4,32,32,128]{3,2,1,0:T(8,128)} %bitcast.2, bf16[192,256]{1,0:T(8,128)(2,1)} %constant.14.clone.fore_x_hbm, bf16[256,192]{1,0:T(8,128)(2,1)} %constant.15.clone.back_x_hbm, bf16[352,256]{1,0:T(8,128)(2,1)} %constant.16.clone.fore_y_hbm, bf16[512,176]{1,0:T(8,128)(2,1)} %constant.17.clone.back_y_hbm, ...), custom_call_target="tpu_custom_call" | custom-call | tf_op jit(solution)/shard_map/whole/pallas_call | solution.py:935
  94.5 0.0 copy-done
  94.5 2.1 %lines.1 = f32[4,32,32,128]{3,2,1,0:T(8,128)} custom-call(f32[2816,128]{1,0:T(8,128)S(1)} %whole.1.modes, bf16[256,256]{1,0:T(8,128)(2,1)S(1)} %copy-done), custom_call_target="tpu_custom_call" | custom-call | tf_op jit(solution)/shard_map/lines/pallas_call | solution.py:967
Async XLA Ops:
  0.0 94.5 %copy-start = (bf16[256,256]{1,0:T(8,128)(2,1)S(1)}, bf16[256,256]{1,0:T(8,128)(2,1)}, u32[]{:S(2)}) copy-start(bf16[256,256]{1,0:T(8,128)(2,1)} %constant.20.clone.back_x) | copy-start | bytes 393220

commit v5 on v4

--- a/solution.py
+++ b/solution.py
@@ -773,7 +773,8 @@
 
                 return carry
 
-            lax.fori_loop(1, slices, go, 0)
+            for i in range(1, slices):
+                go(i, 0)
 
             @pl.when(tm < SCAN)
             def _():
@@ -786,7 +787,8 @@
                     coarse.remote(i, which, True).wait_recv()
                     return carry
 
-                lax.fori_loop(1, slices, go, 0)
+                for i in range(1, slices):
+                    go(i, 0)
                 coarse.local(which).wait()
 
             wait(0)
@@ -817,7 +819,8 @@
                     back.remote(i, which, False).start()
                     return carry
 
-                lax.fori_loop(1, slices, go, 0)
+                for i in range(1, slices):
+                    go(i, 0)
                 back.local(which).start()
 
             send(0)
@@ -844,7 +847,8 @@
 
                     return carry
 
-                lax.fori_loop(1, slices, wait, 0)
+                for i in range(1, slices):
+                    wait(i, 0)
 
                 @pl.when(tm < SCAN)
                 def _():

time: 96.8 us -> 96.6 us (level)
  no operation moved by 1% of the time
where the time goes in v5:
time: 96.6 us; the launch traced here: 96.5 us
  Pallas kernels  96.5 us (100%)
    pallas_call x1, Pallas kernels, on_device(): pl.pallas_call(whole_kernel, name='whole', out_shape=jax.ShapeDtypeStruct...  94.4 us
    pallas_call x1, Pallas kernels, on_device(): pl.pallas_call(lines_kernel, name='lines', grid=(BLOCK // LINES,), out_sh...  2.11 us

profile of v5, /device:TPU:1, one launch (start us, length us, event | category | flops | bytes accessed | tf_op | source)
XLA Modules:
  0.0 96.5 jit_solution(2345765702212211661)
XLA Ops:
  0.0 0.0 copy-start
  0.0 94.4 %whole.1.modes = f32[2816,128]{1,0:T(8,128)S(1)} custom-call(f32[4,32,32,128]{3,2,1,0:T(8,128)} %bitcast.2, bf16[192,256]{1,0:T(8,128)(2,1)} %constant.14.clone.fore_x_hbm, bf16[256,192]{1,0:T(8,128)(2,1)} %constant.15.clone.back_x_hbm, bf16[352,256]{1,0:T(8,128)(2,1)} %constant.16.clone.fore_y_hbm, bf16[512,176]{1,0:T(8,128)(2,1)} %constant.17.clone.back_y_hbm, ...), custom_call_target="tpu_custom_call" | custom-call | tf_op jit(solution)/shard_map/whole/pallas_call | solution.py:939
  94.4 0.0 copy-done
  94.4 2.1 %lines.1 = f32[4,32,32,128]{3,2,1,0:T(8,128)} custom-call(f32[2816,128]{1,0:T(8,128)S(1)} %whole.1.modes, bf16[256,256]{1,0:T(8,128)(2,1)S(1)} %copy-done), custom_call_target="tpu_custom_call" | custom-call | tf_op jit(solution)/shard_map/lines/pallas_call | solution.py:971
Async XLA Ops:
  0.0 94.4 %copy-start = (bf16[256,256]{1,0:T(8,128)(2,1)S(1)}, bf16[256,256]{1,0:T(8,128)(2,1)}, u32[]{:S(2)}) copy-start(bf16[256,256]{1,0:T(8,128)(2,1)} %constant.20.clone.back_x) | copy-start | bytes 393220
